TPU v7x, 32 devices: a whole 2x2x4 slice. The times are simulated.
32 devices in a mesh: gx: 4 (over y, core), gy: 2 (over x), gz: 4 (over z).
Axes of the slice: x: 2, y: 2, z: 4, core: 2. Of those that a mesh axis runs over, the one named last changes fastest.
Arguments:
- positions: float32 [3, 4, 2, 4, 512], P(None, 'gx', 'gy', 'gz'), may hold values from 0 to 16, as said below
- charges: float32 [4, 2, 4, 512], P('gx', 'gy', 'gz'), may hold values from -4 to 4
- atom_types: int32 [4, 2, 4, 512], P('gx', 'gy', 'gz'), may hold values from 0 to 7
- type_table: float32 [3, 8], replicated, may hold values from 0.5 to 2
- live_count: int32 [4, 2, 4], P('gx', 'gy', 'gz'), may hold values from 358 to 512, as said below
- exp_map: float32 [64, 32, 64], P('gx', 'gy', 'gz'), may hold values from -6 to 6
Outputs:
- displacement: float32 [3, 4, 2, 4, 512], P(None, 'gx', 'gy', 'gz')
- last_force: float32 [3, 4, 2, 4, 512], P(None, 'gx', 'gy', 'gz')
- evolved: float32 [64, 32, 64], P('gx', 'gy', 'gz')
Inputs may be any that keep to these rules, and one draw needn't show every extreme that they name: `positions`: each coordinate lies within its cell's brick: 0 to 16, 16, 16 along x, y, z. The live atoms of a cell are its first live_count slots; some cell has all 512 slots live.
All inputs are finite; a program needn't handle non-finite values.
Results may differ from a plain program's by a relative error of at most 0.0003.
Values sent between devices are 32-bit elements; how exact they have to be, the bound alone decides.
A program may use at most 128 MiB of HBM per device.

v0:
```python
import math

import jax
import jax.numpy as jnp
from jax import lax
from jax.sharding import PartitionSpec as P

SPLAT_MARGIN = 3
BLUR_REACH = 2
STEPS = 2


CUTOFF = 10.0
EPSILON = 1e-06
STEP_SIZE = 1.0
FIT_GAIN = 0.2


def padded(cells, sides, width):
    for axis, dim in sides:
        count = lax.axis_size(axis)
        ends = count - 1
        head = lax.slice_in_dim(cells, 0, width, axis=dim)
        tail = lax.slice_in_dim(cells, cells.shape[dim] - width, cells.shape[dim], axis=dim)
        cells = jnp.concatenate(
            [
                lax.ppermute(tail, axis, [(i, (i + 1) % count) for i in range(ends)]),
                cells,
                lax.ppermute(head, axis, [((i + 1) % count, i) for i in range(ends)]),
            ],
            axis=dim,
        )
    return cells


def pack_atoms(positions, charges, atom_types, type_table, live_count):
    type_total = type_table.shape[1]
    onehot = (atom_types[..., None] == jnp.arange(type_total, dtype=jnp.int32)).astype(jnp.float32)
    props = jnp.sum(onehot[None] * type_table[:, None, None, None, None, :], axis=-1)
    slots = lax.broadcasted_iota(jnp.int32, charges.shape, 3)
    living = (slots < live_count[..., None]).astype(jnp.float32)
    return jnp.concatenate([positions, charges[None], props, living[None]], axis=0)


def block_list(nearby, brick_dims):
    channels = nearby.shape[0]
    slot_count = nearby.shape[-1]
    blocks = jnp.transpose(nearby.reshape(channels, 27, slot_count), (1, 0, 2))
    number = jnp.arange(27, dtype=jnp.int32)
    sides = jnp.stack([number // 9 - 1, number // 3 % 3 - 1, number % 3 - 1], axis=1).astype(
        jnp.float32
    )
    offsets = sides * jnp.array(brick_dims, jnp.float32)[None, :]
    centre = (number == 13).astype(jnp.float32)
    return (blocks, offsets, centre)


def geometry(own_atoms, block, offset):
    separation = own_atoms[0:3, :, None] - (block[0:3, None, :] + offset[:, None, None])
    squared = jnp.sum(separation * separation, axis=0)
    smooth_cut = jnp.maximum(1.0 - squared / (CUTOFF * CUTOFF), 0.0)
    return (separation, squared, smooth_cut)


def born_radius(own_atoms, nearby, brick_dims):
    blocks, offsets, centre = block_list(nearby, brick_dims)
    slot_count = own_atoms.shape[1]
    identity_mask = jnp.eye(slot_count, dtype=jnp.float32)

    def born_visit(summed, element):
        block, offset, middle = element
        separation, squared, smooth_cut = geometry(own_atoms, block, offset)
        keep_mask = 1.0 - middle * identity_mask
        weight_term = (
            jnp.exp(-squared / 8.0)
            * smooth_cut
            * smooth_cut
            * keep_mask
            * (block[5] * block[7])[None, :]
        )
        return (summed + jnp.sum(weight_term, axis=1), None)

    summed, unused = lax.scan(
        born_visit, jnp.zeros((slot_count,), jnp.float32), (blocks, offsets, centre)
    )
    return own_atoms[4] + summed


def gb_forces(own_atoms, own_radius, nearby, near_radius, brick_dims):
    blocks, offsets, centre = block_list(nearby, brick_dims)
    slot_count = own_atoms.shape[1]
    identity_mask = jnp.eye(slot_count, dtype=jnp.float32)
    radii = near_radius.reshape(27, slot_count)

    def gb_visit(summed, element):
        block, radius_block, offset, middle = element
        separation, squared, smooth_cut = geometry(own_atoms, block, offset)
        product = own_radius[:, None] * radius_block[None, :]
        fading = jnp.exp(-squared / (4.0 * product))
        inverse = lax.rsqrt(squared + product * fading)
        charge_pair = (
            (own_atoms[3] * own_atoms[7])[:, None]
            * (block[3] * block[7])[None, :]
            * (1.0 - middle * identity_mask)
        )
        slope = (
            -0.5
            * charge_pair
            * (
                -2.0 * smooth_cut / (CUTOFF * CUTOFF) * inverse
                - 0.5
                * smooth_cut
                * smooth_cut
                * inverse
                * inverse
                * inverse
                * (1.0 - 0.25 * fading)
            )
        )
        return (summed - 2.0 * jnp.sum(slope[None] * separation, axis=2), None)

    summed, unused = lax.scan(
        gb_visit, jnp.zeros((3, slot_count), jnp.float32), (blocks, radii, offsets, centre)
    )
    return summed


def profile(coord, start, stop, shift):
    points = jnp.arange(start, stop, dtype=jnp.float32)
    gap = points[None, :] - (coord[:, None] + shift)
    return (jnp.exp(-0.5 * gap * gap), gap)


def window_range(side, length, reach):
    lower = max(side * length - SPLAT_MARGIN, -reach)
    upper = min(side * length + length + SPLAT_MARGIN, length + reach)
    return (lower, upper)


def splat_window(nearby, brick_dims, reach):
    extent = tuple((length + 2 * reach for length in brick_dims))
    density = jnp.zeros(extent, jnp.float32)
    slot_count = nearby.shape[-1]
    for side_x in (-1, 0, 1):
        for side_y in (-1, 0, 1):
            for side_z in (-1, 0, 1):
                block = nearby[:, side_x + 1, side_y + 1, side_z + 1, :]
                low_x, high_x = window_range(side_x, brick_dims[0], reach)
                low_y, high_y = window_range(side_y, brick_dims[1], reach)
                low_z, high_z = window_range(side_z, brick_dims[2], reach)
                profile_x = profile(block[0], low_x, high_x, float(side_x * brick_dims[0]))[0]
                profile_y = profile(block[1], low_y, high_y, float(side_y * brick_dims[1]))[0]
                profile_z = profile(block[2], low_z, high_z, float(side_z * brick_dims[2]))[0]
                mass = block[6] * block[7]
                plane = ((profile_x * mass[:, None])[:, :, None] * profile_y[:, None, :]).reshape(
                    slot_count, -1
                )
                placed = jnp.dot(plane.T, profile_z, precision=lax.Precision.HIGHEST)
                placed = placed.reshape(high_x - low_x, high_y - low_y, high_z - low_z)
                density = density.at[
                    low_x + reach : high_x + reach,
                    low_y + reach : high_y + reach,
                    low_z + reach : high_z + reach,
                ].add(placed)
    return density


def kernel_weights(reach):
    values = [math.exp(-0.5 * (index - reach) ** 2) for index in range(2 * reach + 1)]
    whole = sum(values)
    return [value / whole for value in values]


def blur_trim(widened, reach):
    weights = kernel_weights(BLUR_REACH)
    result = widened
    for axis in range(3):
        length = result.shape[axis] - 2 * reach
        summed = jnp.zeros(result.shape[:axis] + (length,) + result.shape[axis + 1 :], jnp.float32)
        for index in range(len(weights)):
            start = reach - BLUR_REACH + index
            summed = summed + weights[index] * lax.slice_in_dim(
                result, start, start + length, axis=axis
            )
        result = summed
    return result


def correlate(evolved, exp_map):
    return lax.psum(
        (jnp.sum(evolved * evolved), jnp.sum(evolved * exp_map), jnp.sum(exp_map * exp_map)),
        ("gx", "gy", "gz"),
    )


def correlation_slope(evolved, exp_map, sums):
    squares, cross_sum, target = sums
    norm_value = jnp.sqrt((squares + EPSILON) * (target + EPSILON))
    score = cross_sum / norm_value
    return exp_map / norm_value - score * evolved / (squares + EPSILON)


def fit_force(grad_ext, own_atoms, brick_dims, scale):
    margin = SPLAT_MARGIN
    slot_count = own_atoms.shape[1]
    profile_x, gap_x = profile(own_atoms[0], -margin, brick_dims[0] + margin, 0.0)
    profile_y, gap_y = profile(own_atoms[1], -margin, brick_dims[1] + margin, 0.0)
    profile_z, gap_z = profile(own_atoms[2], -margin, brick_dims[2] + margin, 0.0)
    stacked = jnp.concatenate([profile_z, gap_z * profile_z], axis=0)
    inner = jnp.dot(
        grad_ext.reshape(-1, grad_ext.shape[2]), stacked.T, precision=lax.Precision.HIGHEST
    )
    inner = inner.reshape(grad_ext.shape[0], grad_ext.shape[1], 2 * slot_count)
    plain_z = inner[:, :, :slot_count]
    slope_z = inner[:, :, slot_count:]
    plain_y = jnp.einsum("ija,aj->ia", plain_z, profile_y, precision=lax.Precision.HIGHEST)
    turned_y = jnp.einsum("ija,aj->ia", plain_z, gap_y * profile_y, precision=lax.Precision.HIGHEST)
    turned_z = jnp.einsum("ija,aj->ia", slope_z, profile_y, precision=lax.Precision.HIGHEST)
    force = jnp.stack(
        [
            jnp.sum(gap_x * profile_x * plain_y.T, axis=1),
            jnp.sum(profile_x * turned_y.T, axis=1),
            jnp.sum(profile_x * turned_z.T, axis=1),
        ]
    )
    return scale * (own_atoms[6] * own_atoms[7])[None, :] * force


def inside_window(brick_dims, reach):
    extents = (lax.axis_size("gx"), lax.axis_size("gy"), lax.axis_size("gz"))
    places = (lax.axis_index("gx"), lax.axis_index("gy"), lax.axis_index("gz"))
    factors = []
    for axis in range(3):
        coords = places[axis] * brick_dims[axis] + jnp.arange(
            -reach, brick_dims[axis] + reach, dtype=jnp.int32
        )
        factors.append(
            ((coords >= 0) & (coords < brick_dims[axis] * extents[axis])).astype(jnp.float32)
        )
    return factors[0][:, None, None] * factors[1][None, :, None] * factors[2][None, None, :]


def on_device(positions, charges, atom_types, type_table, live_count, exp_map):
    brick_dims = exp_map.shape
    packed = pack_atoms(positions, charges, atom_types, type_table, live_count)
    grid_points = (
        brick_dims[0]
        * brick_dims[1]
        * brick_dims[2]
        * lax.axis_size("gx")
        * lax.axis_size("gy")
        * lax.axis_size("gz")
    )
    scale = FIT_GAIN * float(grid_points)
    frame_reach = BLUR_REACH + SPLAT_MARGIN
    current = positions
    force = jnp.zeros((3, positions.shape[-1]), jnp.float32)
    evolved = jnp.zeros_like(exp_map)
    for step_index in range(STEPS):
        packed = jnp.concatenate([current, packed[3:]], axis=0)
        nearby = padded(packed, (("gx", 1), ("gy", 2), ("gz", 3)), 1)
        own_atoms = packed[:, 0, 0, 0, :]
        radius = born_radius(own_atoms, nearby, brick_dims)
        near_radius = padded(radius.reshape(1, 1, 1, -1), (("gx", 0), ("gy", 1), ("gz", 2)), 1)
        gb_part = gb_forces(own_atoms, radius, nearby, near_radius, brick_dims)
        density = splat_window(nearby, brick_dims, 0)
        widened = padded(density, (("gx", 0), ("gy", 1), ("gz", 2)), BLUR_REACH)
        evolved = blur_trim(widened, BLUR_REACH)
        sums = correlate(evolved, exp_map)
        sensitivity = correlation_slope(evolved, exp_map, sums)
        deeper = padded(sensitivity, (("gx", 0), ("gy", 1), ("gz", 2)), frame_reach)
        grad_ext = blur_trim(deeper, BLUR_REACH) * inside_window(brick_dims, SPLAT_MARGIN)
        fit_part = fit_force(grad_ext, own_atoms, brick_dims, scale)
        force = gb_part + fit_part
        current = current + STEP_SIZE * (own_atoms[7][None, :] * force).reshape(current.shape)
    return (current - positions, force.reshape(current.shape), evolved)


def solution(mesh):
    placed = (
        P(None, "gx", "gy", "gz", None),
        P("gx", "gy", "gz", None),
        P("gx", "gy", "gz", None),
        P(),
        P("gx", "gy", "gz"),
        P("gx", "gy", "gz"),
    )
    return jax.shard_map(
        on_device,
        mesh=mesh,
        in_specs=placed,
        out_specs=(
            P(None, "gx", "gy", "gz", None),
            P(None, "gx", "gy", "gz", None),
            P("gx", "gy", "gz"),
        ),
        check_vma=False,
    )
```

profile of v0, /device:TPU:20, one launch (start us, length us, event | category | flops | bytes accessed | tf_op | source)
XLA Modules:
  0.0 647.1 jit_solution(14812498739205900560)
XLA Ops:
  12.3 2.8 and_reduce_fusion.2
  17.1 4.5 collective-permute-start.2
  26.5 3.5 collective-permute-start.4
  51.9 6.4 scatter-add.191
  65.1 5.0 scatter-add.200
  78.6 3.6 collective-permute-start.13
  83.7 4.3 collective-permute-start.14
  89.4 4.2 collective-permute-done.15
  93.8 3.5 collective-permute-start.16
  99.6 56.6 %while.104 = (s32[]{:T(128)}, f32[512]{0:T(512)S(1)}, f32[8,512]{1,0:T(8,128)S(1)}, f32[27,8,512]{2,1,0:T(8,128)S(1)}, f32[27,3]{1,0:T(8,128)S(1)}, /*index=5*/f32[27]{0:T(128)S(1)}, s32[]{:T(128)}, s32[]{:T(128)}, s32[]{}, s32[]{}) while((s32[]{:T(128)}, f32[512]{0:T(512)S(1)}, f32[8,512]{1,0:T(8,128)S(1)}, ...), condition=%wide.region_4.5_spmd.clone, body=%wide.region_1.4_spmd.clone.sunk | while | flops 5507589 | bytes 2150615 | solution.py:83
  158.4 2.6 collective-permute-start.6
  162.3 40.0 %all-reduce.3 = (f32[]{:T(128)}, f32[]{:T(128)}, f32[]{:T(128)}) all-reduce(f32[]{:T(128)} %get-tuple-element.1175, f32[]{:T(128)} %get-tuple-element.1174, f32[]{:T(128)} %get-tuple-element.1173), channel_id=1, replica_groups=mesh['gx'=4,'gy'=2,'gz'=4] {'gx','gy','gz'}, use_global_device_ids=true, to_apply=%region_13.14 | all-reduce | flops 3 | bytes 24 | tf_op jit(solution)/shard_map/psum | solution.py:190
  206.2 3.6 collective-permute-start.19
  211.2 4.5 collective-permute-start.8
  221.0 3.3 collective-permute-start.10
  226.5 3.9 collective-permute-start.23
  230.6 92.6 %while.105 = (s32[]{:T(128)}, f32[3,512]{1,0:T(4,128)S(1)}, f32[512,1]{0,1:T(1,128)S(1)}, f32[27,8,512]{2,1,0:T(8,128)S(1)}, f32[27]{0:T(128)S(1)}, /*index=5*/f...) while((s32[]{:T(128)}, f32[3,512]{1,0:T(4,128)S(1)}, ...), condition=%wide.region_8.9_spmd.clone, body=%wide.region_5.8_spmd.clone.sunk | while | flops 11539461 | bytes 4286707 | solution.py:122
  335.0 4.6 collective-permute-start.26
  343.9 3.3 collective-permute-start.28
  370.5 6.4 scatter-add.235
  382.8 5.0 scatter-add.244
  396.3 3.6 collective-permute-start.37
  401.4 4.2 collective-permute-start.38
  407.1 4.2 collective-permute-done.39
  411.5 3.3 collective-permute-start.40
  417.4 59.0 %while.106 = (s32[]{:T(128)}, f32[512]{0:T(512)S(1)}, f32[8,512]{1,0:T(8,128)S(1)}, f32[27,8,512]{2,1,0:T(8,128)S(1)}, f32[27,3]{1,0:T(8,128)S(1)}, /*index=5*/f32[27]{0:T(128)S(1)}, s32[]{:T(128)}, s32[]{:T(128)}, s32[]{}, s32[]{}) while((s32[]{:T(128)}, f32[512]{0:T(512)S(1)}, f32[8,512]{1,0:T(8,128)S(1)}, ...), condition=%wide.region_24.25_spmd.clone, body=%wide.region_21.24_spmd.clone.sunk | while | flops 5507589 | bytes 2150615 | solution.py:83
  482.2 39.8 %all-reduce.2 = (f32[]{:T(128)}, f32[]{:T(128)}) all-reduce(f32[]{:T(128)} %get-tuple-element.1172, f32[]{:T(128)} %get-tuple-element.1171), channel_id=1, replica_groups=mesh['gx'=4,'gy'=2,'gz'=4] {'gx','gy','gz'}, use_global_device_ids=true, to_apply=%region_30.31 | all-reduce | flops 2 | bytes 16 | tf_op jit(solution)/shard_map/psum | solution.py:190
  525.3 3.6 collective-permute-start.43
  530.3 4.5 collective-permute-start.32
  540.1 3.3 collective-permute-start.34
  545.7 3.9 collective-permute-start.47
  549.7 92.6 %while.107 = (s32[]{:T(128)}, f32[3,512]{1,0:T(4,128)S(1)}, f32[512,1]{0,1:T(1,128)S(1)}, f32[27,8,512]{2,1,0:T(8,128)S(1)}, f32[27]{0:T(128)S(1)}, /*index=5*/f...) while((s32[]{:T(128)}, f32[3,512]{1,0:T(4,128)S(1)}, ...), condition=%wide.region_28.29_spmd.clone, body=%wide.region_25.28_spmd.clone.sunk | while | flops 11539461 | bytes 4286707 | solution.py:122
  (1463 shorter events, 449.9 us)
Async XLA Ops:
  4.1 10.9 %collective-permute-start.1 = (f32[8,1,1,1,512]{4,0,3,2,1:T(8,128)S(1)}, f32[8,1,1,1,512]{4,0,3,2,1:T(8,128)S(1)}, u32[]{:S(2)}, u32[]{:S(2)}) collective-permute-start(f32[8,1,1,1,512]{4,0,3,2,1:T(8,128)S(1)} %pad_maximum_fusion.31), channel_id=1, source_target_pairs={{8,0},{16,8},{24,16},{9,1},{17,9},{25,17},{10,2},{18,10},{26,18},{... | collective-permute-start | bytes 49160 | tf_op jit(solution)/shard_map/ppermute | solution.py:29
  6.1 9.0 %collective-permute-start = (f32[8,1,1,1,512]{4,0,3,2,1:T(8,128)S(1)}, f32[8,1,1,1,512]{4,0,3,2,1:T(8,128)S(1)}, u32[]{:S(2)}, u32[]{:S(2)}) collective-permute-start(f32[8,1,1,1,512]{4,0,3,2,1:T(8,128)S(1)} %pad_maximum_fusion.31), channel_id=1, source_target_pairs={{0,8},{8,16},{16,24},{1,9},{9,17},{17,25},{2,10},{10,18},{18,26},{... | collective-permute-start | bytes 49160 | tf_op jit(solution)/shard_map/ppermute | solution.py:27
  24.1 7.0 %collective-permute-start.5 = (f32[8,3,3,1,512]{4,0,3,2,1:T(8,128)S(1)}, f32[8,3,3,1,512]{4,0,3,2,1:T(8,128)S(1)}, u32[]{:S(2)}, u32[]{:S(2)}) collective-permute-start(f32[8,3,3,1,512]{4,0,3,2,1:T(8,128)S(1)} %fusion.135), channel_id=1, source_target_pairs={{1,0},{2,1},{3,2},{5,4},{6,5},{7,6},{9,8},{10,9},{11,10},{13,12},{... | collective-permute-start | bytes 442376 | tf_op jit(solution)/shard_map/ppermute | solution.py:29
  26.5 7.0 %collective-permute-start.4 = (f32[8,3,3,1,512]{4,0,3,2,1:T(8,128)S(1)}, f32[8,3,3,1,512]{4,0,3,2,1:T(8,128)S(1)}, u32[]{:S(2)}, u32[]{:S(2)}) collective-permute-start(f32[8,3,3,1,512]{4,0,3,2,1:T(8,128)S(1)} %fusion.135), channel_id=1, source_target_pairs={{0,1},{1,2},{2,3},{4,5},{5,6},{6,7},{8,9},{9,10},{10,11},{12,13},{... | collective-permute-start | bytes 442376 | tf_op jit(solution)/shard_map/ppermute | solution.py:27
  93.8 67.2 %collective-permute-start.16 = (f32[20,20,2]{2,1,0:T(8,128)S(1)}, f32[20,20,2]{2,1,0:T(8,128)S(1)}, u32[]{:S(2)}, u32[]{:S(2)}) collective-permute-start(f32[20,20,2]{2,1,0:T(8,128)S(1)} %get-tuple-element.1257), channel_id=1, source_target_pairs={{0,1},{1,2},{2,3},{4,5},{5,6},{6,7},{8,9},{9,10},{10,11},{12,13},{... | collective-permute-start | bytes 9608 | tf_op jit(solution)/shard_map/ppermute | solution.py:27
  97.3 63.8 %collective-permute-start.17 = (f32[20,20,2]{2,1,0:T(8,128)S(1)}, f32[20,20,2]{2,1,0:T(8,128)S(1)}, u32[]{:S(2)}, u32[]{:S(2)}) collective-permute-start(f32[20,20,2]{2,1,0:T(8,128)S(1)} %get-tuple-element.1258), channel_id=1, source_target_pairs={{1,0},{2,1},{3,2},{5,4},{6,5},{7,6},{9,8},{10,9},{11,10},{13,12},{... | collective-permute-start | bytes 9608 | tf_op jit(solution)/shard_map/ppermute | solution.py:29
  156.3 53.5 %collective-permute-start.7 = (f32[1,1,1,512]{3,2,1,0:T(1,128)S(1)}, f32[1,1,1,512]{3,2,1,0:T(1,128)S(1)}, u32[]{:S(2)}, u32[]{:S(2)}) collective-permute-start(f32[1,1,1,512]{3,2,1,0:T(1,128)S(1)} %bitcast.821), channel_id=1, source_target_pairs={{8,0},{16,8},{24,16},{9,1},{17,9},{25,17},{10,2},{18,10},{26,18},{... | collective-permute-start | bytes 6152 | tf_op jit(solution)/shard_map/ppermute | solution.py:29
  158.4 51.5 %collective-permute-start.6 = (f32[1,1,1,512]{3,2,1,0:T(1,128)S(1)}, f32[1,1,1,512]{3,2,1,0:T(1,128)S(1)}, u32[]{:S(2)}, u32[]{:S(2)}) collective-permute-start(f32[1,1,1,512]{3,2,1,0:T(1,128)S(1)} %bitcast.822), channel_id=1, source_target_pairs={{0,8},{8,16},{16,24},{1,9},{9,17},{17,25},{2,10},{10,18},{18,26},{... | collective-permute-start | bytes 6152 | tf_op jit(solution)/shard_map/ppermute | solution.py:27
  204.3 11.5 %collective-permute-start.18 = (f32[5,16,16]{2,1,0:T(8,128)S(1)}, f32[5,16,16]{2,1,0:T(8,128)S(1)}, u32[]{:S(2)}, u32[]{:S(2)}) collective-permute-start(f32[5,16,16]{2,1,0:T(8,128)S(1)} %get-tuple-element.1415), channel_id=1, source_target_pairs={{0,8},{8,16},{16,24},{1,9},{9,17},{17,25},{2,10},{10,18},{18,26},{... | collective-permute-start | bytes 15368 | tf_op jit(solution)/shard_map/ppermute | solution.py:27
  206.2 9.6 %collective-permute-start.19 = (f32[5,16,16]{2,1,0:T(8,128)S(1)}, f32[5,16,16]{2,1,0:T(8,128)S(1)}, u32[]{:S(2)}, u32[]{:S(2)}) collective-permute-start(f32[5,16,16]{2,1,0:T(8,128)S(1)} %get-tuple-element.1416), channel_id=1, source_target_pairs={{8,0},{16,8},{24,16},{9,1},{17,9},{25,17},{10,2},{18,10},{26,18},{... | collective-permute-start | bytes 15368 | tf_op jit(solution)/shard_map/ppermute | solution.py:29
  209.9 8.5 %collective-permute-start.9 = (f32[3,1,1,512]{3,2,1,0:T(1,128)S(1)}, f32[3,1,1,512]{3,2,1,0:T(1,128)S(1)}, u32[]{:S(2)}, u32[]{:S(2)}) collective-permute-start(f32[3,1,1,512]{3,2,1,0:T(1,128)S(1)} %pad_maximum_fusion.44), channel_id=1, source_target_pairs={{4,0},{5,1},{6,2},{7,3},{12,8},{13,9},{14,10},{15,11},{20,16},{21,... | collective-permute-start | bytes 18440 | tf_op jit(solution)/shard_map/ppermute | solution.py:29
  211.2 7.2 %collective-permute-start.8 = (f32[3,1,1,512]{3,2,1,0:T(1,128)S(1)}, f32[3,1,1,512]{3,2,1,0:T(1,128)S(1)}, u32[]{:S(2)}, u32[]{:S(2)}) collective-permute-start(f32[3,1,1,512]{3,2,1,0:T(1,128)S(1)} %pad_maximum_fusion.44), channel_id=1, source_target_pairs={{0,4},{1,5},{2,6},{3,7},{8,12},{9,13},{10,14},{11,15},{16,20},{17,... | collective-permute-start | bytes 18440 | tf_op jit(solution)/shard_map/ppermute | solution.py:27
  215.8 8.5 %collective-permute-start.20 = (f32[26,5,16]{2,1,0:T(8,128)S(1)}, f32[26,5,16]{2,1,0:T(8,128)S(1)}, u32[]{:S(2)}, u32[]{:S(2)}) collective-permute-start(f32[26,5,16]{2,1,0:T(8,128)S(1)} %get-tuple-element.1261), channel_id=1, source_target_pairs={{0,4},{1,5},{2,6},{3,7},{8,12},{9,13},{10,14},{11,15},{16,20},{17,... | collective-permute-start | bytes 24968 | tf_op jit(solution)/shard_map/ppermute | solution.py:27
  217.1 7.2 %collective-permute-start.21 = (f32[26,5,16]{2,1,0:T(8,128)S(1)}, f32[26,5,16]{2,1,0:T(8,128)S(1)}, u32[]{:S(2)}, u32[]{:S(2)}) collective-permute-start(f32[26,5,16]{2,1,0:T(8,128)S(1)} %get-tuple-element.1262), channel_id=1, source_target_pairs={{4,0},{5,1},{6,2},{7,3},{12,8},{13,9},{14,10},{15,11},{20,16},{21,... | collective-permute-start | bytes 24968 | tf_op jit(solution)/shard_map/ppermute | solution.py:29
  218.5 12.0 %collective-permute-start.11 = (f32[3,3,1,512]{3,2,1,0:T(1,128)S(1)}, f32[3,3,1,512]{3,2,1,0:T(1,128)S(1)}, u32[]{:S(2)}, u32[]{:S(2)}) collective-permute-start(f32[3,3,1,512]{3,2,1,0:T(1,128)S(1)} %pad_maximum_fusion.42), channel_id=1, source_target_pairs={{1,0},{2,1},{3,2},{5,4},{6,5},{7,6},{9,8},{10,9},{11,10},{13,12},{... | collective-permute-start | bytes 55304 | tf_op jit(solution)/shard_map/ppermute | solution.py:29
  221.0 9.5 %collective-permute-start.10 = (f32[3,3,1,512]{3,2,1,0:T(1,128)S(1)}, f32[3,3,1,512]{3,2,1,0:T(1,128)S(1)}, u32[]{:S(2)}, u32[]{:S(2)}) collective-permute-start(f32[3,3,1,512]{3,2,1,0:T(1,128)S(1)} %pad_maximum_fusion.42), channel_id=1, source_target_pairs={{0,1},{1,2},{2,3},{4,5},{5,6},{6,7},{8,9},{9,10},{10,11},{12,13},{... | collective-permute-start | bytes 55304 | tf_op jit(solution)/shard_map/ppermute | solution.py:27
  224.6 98.6 %collective-permute-start.22 = (f32[26,26,5]{2,1,0:T(8,128)S(1)}, f32[26,26,5]{2,1,0:T(8,128)S(1)}, u32[]{:S(2)}, u32[]{:S(2)}) collective-permute-start(f32[26,26,5]{2,1,0:T(8,128)S(1)} %get-tuple-element.1253), channel_id=1, source_target_pairs={{0,1},{1,2},{2,3},{4,5},{5,6},{6,7},{8,9},{9,10},{10,11},{12,13},{... | collective-permute-start | bytes 40568 | tf_op jit(solution)/shard_map/ppermute | solution.py:27
  226.5 96.7 %collective-permute-start.23 = (f32[26,26,5]{2,1,0:T(8,128)S(1)}, f32[26,26,5]{2,1,0:T(8,128)S(1)}, u32[]{:S(2)}, u32[]{:S(2)}) collective-permute-start(f32[26,26,5]{2,1,0:T(8,128)S(1)} %get-tuple-element.1254), channel_id=1, source_target_pairs={{1,0},{2,1},{3,2},{5,4},{6,5},{7,6},{9,8},{10,9},{11,10},{13,12},{... | collective-permute-start | bytes 40568 | tf_op jit(solution)/shard_map/ppermute | solution.py:29
  411.5 69.4 %collective-permute-start.40 = (f32[20,20,2]{2,1,0:T(8,128)S(1)}, f32[20,20,2]{2,1,0:T(8,128)S(1)}, u32[]{:S(2)}, u32[]{:S(2)}) collective-permute-start(f32[20,20,2]{2,1,0:T(8,128)S(1)} %get-tuple-element.1255), channel_id=1, source_target_pairs={{0,1},{1,2},{2,3},{4,5},{5,6},{6,7},{8,9},{9,10},{10,11},{12,13},{... | collective-permute-start | bytes 9608 | tf_op jit(solution)/shard_map/ppermute | solution.py:27
  414.8 66.2 %collective-permute-start.41 = (f32[20,20,2]{2,1,0:T(8,128)S(1)}, f32[20,20,2]{2,1,0:T(8,128)S(1)}, u32[]{:S(2)}, u32[]{:S(2)}) collective-permute-start(f32[20,20,2]{2,1,0:T(8,128)S(1)} %get-tuple-element.1256), channel_id=1, source_target_pairs={{1,0},{2,1},{3,2},{5,4},{6,5},{7,6},{9,8},{10,9},{11,10},{13,12},{... | collective-permute-start | bytes 9608 | tf_op jit(solution)/shard_map/ppermute | solution.py:29
  476.4 52.5 %collective-permute-start.31 = (f32[1,1,1,512]{3,2,1,0:T(1,128)S(1)}, f32[1,1,1,512]{3,2,1,0:T(1,128)S(1)}, u32[]{:S(2)}, u32[]{:S(2)}) collective-permute-start(f32[1,1,1,512]{3,2,1,0:T(1,128)S(1)} %bitcast.816), channel_id=1, source_target_pairs={{8,0},{16,8},{24,16},{9,1},{17,9},{25,17},{10,2},{18,10},{26,18},{... | collective-permute-start | bytes 6152 | tf_op jit(solution)/shard_map/ppermute | solution.py:29
  478.3 50.6 %collective-permute-start.30 = (f32[1,1,1,512]{3,2,1,0:T(1,128)S(1)}, f32[1,1,1,512]{3,2,1,0:T(1,128)S(1)}, u32[]{:S(2)}, u32[]{:S(2)}) collective-permute-start(f32[1,1,1,512]{3,2,1,0:T(1,128)S(1)} %bitcast.817), channel_id=1, source_target_pairs={{0,8},{8,16},{16,24},{1,9},{9,17},{17,25},{2,10},{10,18},{18,26},{... | collective-permute-start | bytes 6152 | tf_op jit(solution)/shard_map/ppermute | solution.py:27
  523.3 11.5 %collective-permute-start.42 = (f32[5,16,16]{2,1,0:T(8,128)S(1)}, f32[5,16,16]{2,1,0:T(8,128)S(1)}, u32[]{:S(2)}, u32[]{:S(2)}) collective-permute-start(f32[5,16,16]{2,1,0:T(8,128)S(1)} %get-tuple-element.1411), channel_id=1, source_target_pairs={{0,8},{8,16},{16,24},{1,9},{9,17},{17,25},{2,10},{10,18},{18,26},{... | collective-permute-start | bytes 15368 | tf_op jit(solution)/shard_map/ppermute | solution.py:27
  525.3 9.6 %collective-permute-start.43 = (f32[5,16,16]{2,1,0:T(8,128)S(1)}, f32[5,16,16]{2,1,0:T(8,128)S(1)}, u32[]{:S(2)}, u32[]{:S(2)}) collective-permute-start(f32[5,16,16]{2,1,0:T(8,128)S(1)} %get-tuple-element.1412), channel_id=1, source_target_pairs={{8,0},{16,8},{24,16},{9,1},{17,9},{25,17},{10,2},{18,10},{26,18},{... | collective-permute-start | bytes 15368 | tf_op jit(solution)/shard_map/ppermute | solution.py:29
  529.0 8.5 %collective-permute-start.33 = (f32[3,1,1,512]{3,2,1,0:T(1,128)S(1)}, f32[3,1,1,512]{3,2,1,0:T(1,128)S(1)}, u32[]{:S(2)}, u32[]{:S(2)}) collective-permute-start(f32[3,1,1,512]{3,2,1,0:T(1,128)S(1)} %pad_maximum_fusion.45), channel_id=1, source_target_pairs={{4,0},{5,1},{6,2},{7,3},{12,8},{13,9},{14,10},{15,11},{20,16},{21,... | collective-permute-start | bytes 18440 | tf_op jit(solution)/shard_map/ppermute | solution.py:29
  530.3 7.2 %collective-permute-start.32 = (f32[3,1,1,512]{3,2,1,0:T(1,128)S(1)}, f32[3,1,1,512]{3,2,1,0:T(1,128)S(1)}, u32[]{:S(2)}, u32[]{:S(2)}) collective-permute-start(f32[3,1,1,512]{3,2,1,0:T(1,128)S(1)} %pad_maximum_fusion.45), channel_id=1, source_target_pairs={{0,4},{1,5},{2,6},{3,7},{8,12},{9,13},{10,14},{11,15},{16,20},{17,... | collective-permute-start | bytes 18440 | tf_op jit(solution)/shard_map/ppermute | solution.py:27
  534.9 8.5 %collective-permute-start.44 = (f32[26,5,16]{2,1,0:T(8,128)S(1)}, f32[26,5,16]{2,1,0:T(8,128)S(1)}, u32[]{:S(2)}, u32[]{:S(2)}) collective-permute-start(f32[26,5,16]{2,1,0:T(8,128)S(1)} %get-tuple-element.1259), channel_id=1, source_target_pairs={{0,4},{1,5},{2,6},{3,7},{8,12},{9,13},{10,14},{11,15},{16,20},{17,... | collective-permute-start | bytes 24968 | tf_op jit(solution)/shard_map/ppermute | solution.py:27
  536.2 7.2 %collective-permute-start.45 = (f32[26,5,16]{2,1,0:T(8,128)S(1)}, f32[26,5,16]{2,1,0:T(8,128)S(1)}, u32[]{:S(2)}, u32[]{:S(2)}) collective-permute-start(f32[26,5,16]{2,1,0:T(8,128)S(1)} %get-tuple-element.1260), channel_id=1, source_target_pairs={{4,0},{5,1},{6,2},{7,3},{12,8},{13,9},{14,10},{15,11},{20,16},{21,... | collective-permute-start | bytes 24968 | tf_op jit(solution)/shard_map/ppermute | solution.py:29
  537.5 12.0 %collective-permute-start.35 = (f32[3,3,1,512]{3,2,1,0:T(1,128)S(1)}, f32[3,3,1,512]{3,2,1,0:T(1,128)S(1)}, u32[]{:S(2)}, u32[]{:S(2)}) collective-permute-start(f32[3,3,1,512]{3,2,1,0:T(1,128)S(1)} %pad_maximum_fusion.43), channel_id=1, source_target_pairs={{1,0},{2,1},{3,2},{5,4},{6,5},{7,6},{9,8},{10,9},{11,10},{13,12},{... | collective-permute-start | bytes 55304 | tf_op jit(solution)/shard_map/ppermute | solution.py:29
  540.1 9.5 %collective-permute-start.34 = (f32[3,3,1,512]{3,2,1,0:T(1,128)S(1)}, f32[3,3,1,512]{3,2,1,0:T(1,128)S(1)}, u32[]{:S(2)}, u32[]{:S(2)}) collective-permute-start(f32[3,3,1,512]{3,2,1,0:T(1,128)S(1)} %pad_maximum_fusion.43), channel_id=1, source_target_pairs={{0,1},{1,2},{2,3},{4,5},{5,6},{6,7},{8,9},{9,10},{10,11},{12,13},{... | collective-permute-start | bytes 55304 | tf_op jit(solution)/shard_map/ppermute | solution.py:27
  543.7 98.6 %collective-permute-start.46 = (f32[26,26,5]{2,1,0:T(8,128)S(1)}, f32[26,26,5]{2,1,0:T(8,128)S(1)}, u32[]{:S(2)}, u32[]{:S(2)}) collective-permute-start(f32[26,26,5]{2,1,0:T(8,128)S(1)} %get-tuple-element.1251), channel_id=1, source_target_pairs={{0,1},{1,2},{2,3},{4,5},{5,6},{6,7},{8,9},{9,10},{10,11},{12,13},{... | collective-permute-start | bytes 40568 | tf_op jit(solution)/shard_map/ppermute | solution.py:27
  545.7 96.7 %collective-permute-start.47 = (f32[26,26,5]{2,1,0:T(8,128)S(1)}, f32[26,26,5]{2,1,0:T(8,128)S(1)}, u32[]{:S(2)}, u32[]{:S(2)}) collective-permute-start(f32[26,26,5]{2,1,0:T(8,128)S(1)} %get-tuple-element.1252), channel_id=1, source_target_pairs={{1,0},{2,1},{3,2},{5,4},{6,5},{7,6},{9,8},{10,9},{11,10},{13,12},{... | collective-permute-start | bytes 40568 | tf_op jit(solution)/shard_map/ppermute | solution.py:29
  (20 other events, 197.8 us)
where the time goes:
time: 655 us; the launch traced here: 647 us
  other arithmetic  254 us (39%)
  local copies, waits for them, and re-layouts  126 us (19%)
  starting transfers between devices  126 us (19%)
  blocking collectives  79.8 us (12%)
  matrix products  28.6 us (4%)
  waiting for transfers between devices  20.6 us (3%)
  between operations  7.75 us (1%)
    mul x54, other arithmetic, gb_visit(): -0.5 * charge_pair  92.2 us
    psum x2, blocking collectives, correlate(): lax.psum((jnp.sum(evolved * evolved), jnp.sum(evolved * exp_map), jnp.sum...  79.8 us
    ppermute x24, starting transfers between devices, padded(): lax.ppermute(tail, axis, [(i, (i + 1) % count) for i in range(ends)])  70.9 us
    dynamic_slice x108, local copies, waits for them, and re-layouts, born_radius(): lax.scan(born_visit, jnp.zeros((slot_count,), jnp.float32), (blocks, offs...  63.1 us
    reduce_sum x54, other arithmetic, born_visit(): return (summed + jnp.sum(weight_term, axis=1), None)  57.6 us
    ppermute x24, starting transfers between devices, padded(): lax.ppermute(head, axis, [((i + 1) % count, i) for i in range(ends)])  55.5 us
    scatter-add x50, local copies, waits for them, and re-layouts, splat_window(): density = density.at[low_x + reach:high_x + reach, low_y + reach:high_y +...  54 us
    reduce_sum x108, other arithmetic, geometry(): squared = jnp.sum(separation * separation, axis=0)  39.2 us
  transfers between devices with their start and end apart: 48, of which 13 were waited for; matrix products, arithmetic and copies ran while one was open for 48% of the time, Pallas kernels for 0%

commit v1 on v0

v1 whole, which is shorter than its diff:
```python
import functools
import math

import jax
import jax.numpy as jnp
from jax import lax
from jax.experimental import pallas as pl
from jax.experimental.pallas import tpu as pltpu
from jax.sharding import PartitionSpec as P

SPLAT_MARGIN = 3
BLUR_REACH = 2
STEPS = 2
CUTOFF = 10.0
EPSILON = 1e-06
STEP_SIZE = 1.0
FIT_GAIN = 0.2
REACH = SPLAT_MARGIN + BLUR_REACH
PAD = 8
LANES = 128
ROWS = 64
MESH = pl.DeviceIdType.MESH
AXES = ("gx", "gy", "gz")
VMEM = pl.BlockSpec(memory_space=pltpu.VMEM)
SMEM = pl.BlockSpec(memory_space=pltpu.SMEM)


def sides_of(number):
    return (number // 9 - 1, number // 3 % 3 - 1, number % 3 - 1)


def exchange_kernel(sizes, count, everyone, *refs):
    sources = refs[:count]
    position = count
    if everyone:
        part_ref = refs[position]
        position += 1
    outs = refs[position : position + count]
    position += count
    if everyone:
        parts_out = refs[position]
        position += 1
    send, recv = refs[position : position + 2]
    me = tuple(lax.axis_index(axis) for axis in AXES)
    total = sizes[0] * sizes[1] * sizes[2]
    mine = (me[0] * sizes[1] + me[1]) * sizes[2] + me[2]

    def exists(number):
        sides = sides_of(number)
        inside = None
        for axis in range(3):
            place = me[axis] + sides[axis]
            good = (place >= 0) & (place < sizes[axis])
            inside = good if inside is None else inside & good
        return inside

    def target(number):
        sides = sides_of(number)
        return tuple(me[axis] + sides[axis] for axis in range(3))

    def device_at(linear):
        return (
            linear // (sizes[1] * sizes[2]),
            linear // sizes[2] % sizes[1],
            linear % sizes[2],
        )

    others = [number for number in range(27) if number != 13]
    barrier = pltpu.get_barrier_semaphore()
    if everyone:

        def greet(step, carry):
            linear = lax.rem(mine + step, total)
            pl.semaphore_signal(barrier, inc=1, device_id=device_at(linear), device_id_type=MESH)
            return carry

        lax.fori_loop(1, total, greet, 0)
        pl.semaphore_wait(barrier, total - 1)
        send_all, recv_all = refs[position + 2 : position + 4]
    else:
        expected = 1
        for axis in range(3):
            low = jnp.where(me[axis] > 0, 1, 0)
            high = jnp.where(me[axis] < sizes[axis] - 1, 1, 0)
            expected = expected * (1 + low + high)
        for number in others:

            @pl.when(exists(number))
            def _(number=number):
                pl.semaphore_signal(barrier, inc=1, device_id=target(number), device_id_type=MESH)

        pl.semaphore_wait(barrier, expected - 1)

    def outgoing(index, number):
        return pltpu.make_async_remote_copy(
            src_ref=sources[index],
            dst_ref=outs[index].at[26 - number],
            send_sem=send.at[index, number],
            recv_sem=recv.at[index, 26 - number],
            device_id=target(number),
            device_id_type=MESH,
        )

    def arriving(index, number):
        return pltpu.make_async_remote_copy(
            src_ref=sources[index],
            dst_ref=outs[index].at[number],
            send_sem=send.at[index, number],
            recv_sem=recv.at[index, number],
            device_id=target(number),
            device_id_type=MESH,
        )

    def sum_copy(linear, slot):
        return pltpu.make_async_remote_copy(
            src_ref=part_ref,
            dst_ref=parts_out.at[slot],
            send_sem=send_all.at[linear],
            recv_sem=recv_all.at[slot],
            device_id=device_at(linear),
            device_id_type=MESH,
        )

    if everyone:

        def send_sum(step, carry):
            sum_copy(lax.rem(mine + step, total), mine).start()
            return carry

        lax.fori_loop(1, total, send_sum, 0)
    for number in others:

        @pl.when(exists(number))
        def _(number=number):
            for index in range(count):
                outgoing(index, number).start()

    for index in range(count):
        outs[index][13] = sources[index][...]
    if everyone:
        parts_out[mine] = part_ref[...]
    for number in others:

        @pl.when(jnp.logical_not(exists(number)))
        def _(number=number):
            for index in range(count):
                outs[index][number] = jnp.zeros(sources[index].shape, jnp.float32)

    for number in others:

        @pl.when(exists(number))
        def _(number=number):
            for index in range(count):
                outgoing(index, number).wait_send()
                arriving(index, number).wait_recv()

    if everyone:

        def wait_sum(step, carry):
            linear = lax.rem(mine + step, total)
            sum_copy(linear, mine).wait_send()
            sum_copy(linear, linear).wait_recv()
            return carry

        lax.fori_loop(1, total, wait_sum, 0)


def exchange(arrays, part, collective_id):
    sizes = tuple(lax.axis_size(axis) for axis in AXES)
    total = sizes[0] * sizes[1] * sizes[2]
    count = len(arrays)
    everyone = part is not None
    out_shape = [jax.ShapeDtypeStruct((27,) + a.shape, jnp.float32) for a in arrays]
    scratch = [pltpu.SemaphoreType.DMA((count, 27)), pltpu.SemaphoreType.DMA((count, 27))]
    operands = list(arrays)
    if everyone:
        operands.append(part)
        out_shape.append(jax.ShapeDtypeStruct((total,) + part.shape, jnp.float32))
        scratch += [pltpu.SemaphoreType.DMA((total,)), pltpu.SemaphoreType.DMA((total,))]
    return pl.pallas_call(
        functools.partial(exchange_kernel, sizes, count, everyone),
        out_shape=out_shape,
        in_specs=[VMEM] * len(operands),
        out_specs=[VMEM] * len(out_shape),
        scratch_shapes=scratch,
        compiler_params=pltpu.CompilerParams(collective_id=collective_id, has_side_effects=True),
        name=f"exchange{collective_id}",
    )(*operands)


def kernel_weights(reach):
    values = [math.exp(-0.5 * (index - reach) ** 2) for index in range(2 * reach + 1)]
    whole = sum(values)
    return [value / whole for value in values]


def spread(values):
    weights = kernel_weights(BLUR_REACH)
    rows = values.shape[0]
    result = weights[BLUR_REACH] * values
    for shift in range(1, BLUR_REACH + 1):
        both = pltpu.roll(values, shift, 0) + pltpu.roll(values, rows - shift, 0)
        result = result + weights[BLUR_REACH + shift] * both
    return result


def profile_rows(coord, side, length, place, extent, slope):
    rows = length + 2 * PAD
    point = lax.broadcasted_iota(jnp.int32, (rows, coord.shape[-1]), 0) - PAD
    within = point + place * length
    start = side * length
    grid = (within >= 0) & (within < extent * length)
    window = grid & (point >= start - SPLAT_MARGIN) & (point < start + length + SPLAT_MARGIN)
    reach = grid & (point >= start - REACH) & (point < start + length + REACH)
    offset = jnp.asarray(side * length, jnp.float32)
    gap = point.astype(jnp.float32) - (coord + offset)
    plain = jnp.where(window, jnp.exp(-0.5 * gap * gap), 0.0)
    wide = jnp.where(reach, spread(plain), 0.0)
    if not slope:
        return wide
    return wide, jnp.where(reach, spread(gap * plain), 0.0)


def born_kernel(dims, near_ref, own_ref, list_ref, count_ref, out_ref):
    slots = near_ref.shape[-1]
    pieces = slots // LANES

    def block(index, carry):
        base = pl.multiple_of(index * ROWS, ROWS)
        own = [
            jnp.broadcast_to(own_ref[pl.ds(base, ROWS), k : k + 1], (ROWS, LANES))
            for k in range(3)
        ]

        def visit(step, summed):
            number = list_ref[index, step]
            cell = number // pieces
            lane = pl.multiple_of(number % pieces * LANES, LANES)
            sides = sides_of(cell)
            squared = None
            for axis in range(3):
                row = near_ref[cell, axis : axis + 1, pl.ds(lane, LANES)]
                shift = sides[axis].astype(jnp.float32) * float(dims[axis])
                gap = own[axis] - (row + shift)
                squared = gap * gap if squared is None else squared + gap * gap
            smooth = jnp.maximum(1.0 - squared * (1.0 / (CUTOFF * CUTOFF)), 0.0)
            weight = near_ref[cell, 4:5, pl.ds(lane, LANES)]
            return summed + jnp.exp(squared * -0.125) * (smooth * smooth) * weight

        summed = lax.fori_loop(
            0, count_ref[0, index], visit, jnp.zeros((ROWS, LANES), jnp.float32)
        )
        own_screen = own_ref[pl.ds(base, ROWS), 4:5]
        radius = own_ref[pl.ds(base, ROWS), 6:7]
        out_ref[pl.ds(base, ROWS), :] = radius + (
            jnp.sum(summed, axis=1, keepdims=True) - own_screen
        )
        return carry

    lax.fori_loop(0, slots // ROWS, block, 0)


def force_kernel(dims, near_ref, radii_ref, own_ref, radius_ref, list_ref, count_ref, out_ref):
    slots = near_ref.shape[-1]
    pieces = slots // LANES

    def block(index, carry):
        base = pl.multiple_of(index * ROWS, ROWS)
        own = [
            jnp.broadcast_to(own_ref[pl.ds(base, ROWS), k : k + 1], (ROWS, LANES))
            for k in range(3)
        ]
        radius = jnp.broadcast_to(radius_ref[pl.ds(base, ROWS), :], (ROWS, LANES))
        inverse_radius = -0.25 / radius

        def visit(step, summed):
            number = list_ref[index, step]
            cell = number // pieces
            lane = pl.multiple_of(number % pieces * LANES, LANES)
            sides = sides_of(cell)
            squared = None
            gaps = []
            for axis in range(3):
                row = near_ref[cell, axis : axis + 1, pl.ds(lane, LANES)]
                shift = sides[axis].astype(jnp.float32) * float(dims[axis])
                gap = own[axis] - (row + shift)
                gaps.append(gap)
                squared = gap * gap if squared is None else squared + gap * gap
            smooth = jnp.maximum(1.0 - squared * (1.0 / (CUTOFF * CUTOFF)), 0.0)
            near_radius = radii_ref[cell, :, pl.ds(lane, LANES)]
            charge = near_ref[cell, 3:4, pl.ds(lane, LANES)]
            fading = jnp.exp(squared * (inverse_radius * (1.0 / near_radius)))
            inverse = lax.rsqrt(squared + (radius * near_radius) * fading)
            common = (
                (charge * (smooth * inverse))
                * (
                    2.0 / (CUTOFF * CUTOFF)
                    + (smooth * (inverse * inverse)) * (0.5 - 0.125 * fading)
                )
            )
            return tuple(total + common * gap for total, gap in zip(summed, gaps))

        zero = jnp.zeros((ROWS, LANES), jnp.float32)
        summed = lax.fori_loop(0, count_ref[0, index], visit, (zero, zero, zero))
        charge = own_ref[pl.ds(base, ROWS), 3:4]
        for axis in range(3):
            out_ref[pl.ds(base, ROWS), axis : axis + 1] = -charge * jnp.sum(
                summed[axis], axis=1, keepdims=True
            )
        return carry

    lax.fori_loop(0, slots // ROWS, block, 0)


def halves(value):
    high = value.astype(jnp.bfloat16)
    return high, (value - high.astype(jnp.float32)).astype(jnp.bfloat16)


def evolved_kernel(dims, sizes, near_ref, place_ref, out_ref, px_ref, py_ref, pz_ref, total_ref):
    places = [place_ref[0, k] for k in range(3)]
    depth = dims[2] + 2 * PAD

    def profiles(cell, carry):
        sides = sides_of(cell)
        made = [
            profile_rows(
                near_ref[cell, axis : axis + 1, :],
                sides[axis],
                dims[axis],
                places[axis],
                sizes[axis],
                False,
            )
            for axis in range(3)
        ]
        px_ref[cell] = made[0] * near_ref[cell, 5:6, :]
        py_ref[cell] = made[1]
        high, low = halves(made[2])
        pz_ref[cell, 0:depth, :] = high
        pz_ref[cell, depth : 2 * depth, :] = low
        return carry

    lax.fori_loop(0, 27, profiles, 0)
    half_x = dims[0] // 2 + REACH
    half_y = dims[1] // 2 + PAD
    rows = half_x * half_y
    for hx in range(2):
        first = PAD - REACH if hx == 0 else PAD + dims[0] // 2
        for hy in range(2):
            total_ref[...] = jnp.zeros_like(total_ref)

            def add(step, carry):
                cell = (hx + step // 6) * 9 + (hy + step // 3 % 2) * 3 + step % 3
                py = py_ref[cell, hy * half_y : (hy + 1) * half_y, :]
                pieces_high, pieces_low = [], []
                for k in range(half_x):
                    high, low = halves(px_ref[cell, first + k : first + k + 1, :] * py)
                    pieces_high.append(high)
                    pieces_low.append(low)
                plane = jnp.concatenate(pieces_high + pieces_low, axis=0)
                total_ref[...] += lax.dot_general(
                    plane,
                    pz_ref[cell],
                    (((1,), (1,)), ((), ())),
                    preferred_element_type=jnp.float32,
                )
                return carry

            lax.fori_loop(0, 12, add, 0)
            result = (
                total_ref[0:rows, 0:depth]
                + total_ref[0:rows, depth : 2 * depth]
                + total_ref[rows : 2 * rows, 0:depth]
            )
            out_ref[
                hx * half_x : (hx + 1) * half_x, hy * half_y : (hy + 1) * half_y, :
            ] = result.reshape(half_x, half_y, depth)


def fit_kernel(dims, sizes, own_ref, place_ref, sens_ref, out_ref, big_ref):
    places = [place_ref[0, k] for k in range(3)]
    slots = own_ref.shape[-1]
    wide = []
    slope = []
    for axis in range(3):
        a, b = profile_rows(
            own_ref[axis : axis + 1, :], 0, dims[axis], places[axis], sizes[axis], True
        )
        wide.append(a)
        slope.append(b)
    both = jnp.concatenate([wide[2], slope[2]], axis=1)
    high, low = halves(both)
    right = jnp.concatenate([high, low, high], axis=0)
    big_ref[...] = jnp.dot(sens_ref[...], right, preferred_element_type=jnp.float32)
    height = dims[1] + 2 * PAD
    force = [jnp.zeros((1, slots), jnp.float32) for _ in range(3)]
    for k in range(dims[0] + 2 * REACH):
        row = PAD - REACH + k
        plain_z = big_ref[k * height : (k + 1) * height, 0:slots]
        slope_z = big_ref[k * height : (k + 1) * height, slots : 2 * slots]
        plain = jnp.sum(plain_z * wide[1], axis=0, keepdims=True)
        turned_y = jnp.sum(plain_z * slope[1], axis=0, keepdims=True)
        turned_z = jnp.sum(slope_z * wide[1], axis=0, keepdims=True)
        here = wide[0][row : row + 1, :]
        force[0] = force[0] + slope[0][row : row + 1, :] * plain
        force[1] = force[1] + here * turned_y
        force[2] = force[2] + here * turned_z
    mass = own_ref[5:6, :]
    for axis in range(3):
        out_ref[axis : axis + 1, :] = mass * force[axis]


def frame_map(bricks, dims):
    reaches = (REACH, PAD, PAD)
    cube = bricks.reshape((3, 3, 3) + dims)

    def join(parts, axis):
        length = dims[axis]
        return jnp.concatenate(
            [
                lax.slice_in_dim(parts[0], length - reaches[axis], length, axis=axis),
                parts[1],
                lax.slice_in_dim(parts[2], 0, reaches[axis], axis=axis),
            ],
            axis=axis,
        )

    return join(
        [join([join([cube[a, b, c] for c in range(3)], 2) for b in range(3)], 1) for a in range(3)],
        0,
    )


def active_lists(near, dims):
    slots = near.shape[-1]
    pieces = slots // LANES
    blocks = slots // ROWS
    number = jnp.arange(27, dtype=jnp.int32)
    sides = jnp.stack(sides_of(number), axis=1).astype(jnp.float32)
    offsets = sides * jnp.array(dims, jnp.float32)[None, :]
    coords = near[:, 0:3, :] + offsets[:, :, None]
    live = near[:, 7:8, :] > 0.5
    big = 1e30
    low = jnp.where(live, coords, big).reshape(27, 3, pieces, LANES).min(axis=-1)
    high = jnp.where(live, coords, -big).reshape(27, 3, pieces, LANES).max(axis=-1)
    own_low = jnp.where(live[13], coords[13], big).reshape(3, blocks, ROWS).min(axis=-1)
    own_high = jnp.where(live[13], coords[13], -big).reshape(3, blocks, ROWS).max(axis=-1)
    apart = jnp.maximum(
        low[:, :, :, None] - own_high[None, :, None, :],
        own_low[None, :, None, :] - high[:, :, :, None],
    )
    apart = jnp.maximum(apart, 0.0)
    keep = jnp.sum(apart * apart, axis=1) < CUTOFF * CUTOFF * 1.001
    keep = keep.reshape(27 * pieces, blocks).T
    whole = 27 * pieces
    index = jnp.arange(whole, dtype=jnp.int32)
    before = (index[:, None] <= index[None, :]).astype(jnp.bfloat16)
    spot = jnp.dot(
        keep.astype(jnp.bfloat16), before, preferred_element_type=jnp.float32
    ).astype(jnp.int32)
    counts = spot[:, -1]
    chosen = keep[:, :, None] & (spot[:, :, None] - 1 == index[None, None, :])
    lists = jnp.sum(jnp.where(chosen, index[None, :, None], 0), axis=1)
    return lists, counts[None, :]


def on_device(positions, charges, atom_types, type_table, live_count, exp_map):
    dims = exp_map.shape
    sizes = tuple(lax.axis_size(axis) for axis in AXES)
    slots = positions.shape[-1]
    grid_points = dims[0] * dims[1] * dims[2] * sizes[0] * sizes[1] * sizes[2]
    scale = FIT_GAIN * float(grid_points)
    place = jnp.stack([lax.axis_index(axis) for axis in AXES]).astype(jnp.int32).reshape(1, 3)

    kinds = jnp.arange(type_table.shape[1], dtype=jnp.int32)
    onehot = (atom_types.reshape(1, slots) == kinds[:, None]).astype(jnp.float32)
    props = jnp.sum(type_table[:, :, None] * onehot[None], axis=1)
    living = (
        lax.broadcasted_iota(jnp.int32, (1, slots), 1) < live_count.reshape(1, 1)
    ).astype(jnp.float32)
    start = positions.reshape(3, slots)
    fixed = jnp.concatenate(
        [
            charges.reshape(1, slots) * living,
            props[1:2] * living,
            props[2:3] * living,
            props[0:1],
            living,
        ],
        axis=0,
    )
    current = start
    target = jnp.sum(exp_map * exp_map)
    framed = None
    for step in range(STEPS):
        own = jnp.concatenate([current, fixed], axis=0)
        if step == 0:
            near, bricks = exchange([own, exp_map.reshape(-1, LANES)], None, 0)
            framed = frame_map(bricks, dims)
        else:
            (near,) = exchange([own], None, 1)
        columns = own.T
        lists, counts = active_lists(near, dims)
        radius = pl.pallas_call(
            functools.partial(born_kernel, dims),
            out_shape=jax.ShapeDtypeStruct((slots, 1), jnp.float32),
            in_specs=[VMEM, VMEM, SMEM, SMEM],
            out_specs=VMEM,
            name="born",
        )(near, columns, lists, counts)
        wide = pl.pallas_call(
            functools.partial(evolved_kernel, dims, sizes),
            out_shape=jax.ShapeDtypeStruct(
                (dims[0] + 2 * REACH, dims[1] + 2 * PAD, dims[2] + 2 * PAD), jnp.float32
            ),
            in_specs=[VMEM, SMEM],
            out_specs=VMEM,
            scratch_shapes=[
                pltpu.VMEM((27, dims[0] + 2 * PAD, slots), jnp.float32),
                pltpu.VMEM((27, dims[1] + 2 * PAD, slots), jnp.float32),
                pltpu.VMEM((27, 2 * (dims[2] + 2 * PAD), slots), jnp.bfloat16),
                pltpu.VMEM(
                    (
                        2 * (dims[0] // 2 + REACH) * (dims[1] // 2 + PAD),
                        2 * (dims[2] + 2 * PAD),
                    ),
                    jnp.float32,
                ),
            ],
            name="evolve",
        )(near, place)
        evolved = wide[
            REACH : REACH + dims[0], PAD : PAD + dims[1], PAD : PAD + dims[2]
        ]
        lane = lax.broadcasted_iota(jnp.int32, (1, LANES), 1)
        part = jnp.where(
            lane == 0,
            jnp.sum(evolved * evolved),
            jnp.where(lane == 1, jnp.sum(evolved * exp_map), jnp.where(lane == 2, target, 0.0)),
        )
        near_radius, parts = exchange([radius.reshape(1, slots)], part, 2)
        sums = jnp.sum(parts, axis=(0, 1))
        squares, cross_sum, whole_target = sums[0], sums[1], sums[2]
        norm = jnp.sqrt((squares + EPSILON) * (whole_target + EPSILON))
        score = cross_sum / norm
        sensitivity = framed / norm - score * wide / (squares + EPSILON)
        sensitivity = sensitivity.reshape(-1, sensitivity.shape[-1])
        rounded = lax.reduce_precision(sensitivity, 8, 7)
        high, low = rounded.astype(jnp.bfloat16), (sensitivity - rounded).astype(jnp.bfloat16)
        stacked = jnp.concatenate([high, high, low], axis=1)
        fit = pl.pallas_call(
            functools.partial(fit_kernel, dims, sizes),
            out_shape=jax.ShapeDtypeStruct((3, slots), jnp.float32),
            in_specs=[VMEM, SMEM, VMEM],
            out_specs=VMEM,
            scratch_shapes=[pltpu.VMEM((stacked.shape[0], 2 * slots), jnp.float32)],
            name="fit",
        )(own, place, stacked)
        pair = pl.pallas_call(
            functools.partial(force_kernel, dims),
            out_shape=jax.ShapeDtypeStruct((slots, 3), jnp.float32),
            in_specs=[VMEM, VMEM, VMEM, VMEM, SMEM, SMEM],
            out_specs=VMEM,
            name="pair",
        )(near, near_radius, columns, radius, lists, counts)
        force = pair.T + scale * fit
        current = current + STEP_SIZE * (living * force)
    shape = positions.shape
    return ((current - start).reshape(shape), force.reshape(shape), evolved)


def solution(mesh):
    placed = (
        P(None, "gx", "gy", "gz", None),
        P("gx", "gy", "gz", None),
        P("gx", "gy", "gz", None),
        P(),
        P("gx", "gy", "gz"),
        P("gx", "gy", "gz"),
    )
    return jax.shard_map(
        on_device,
        mesh=mesh,
        in_specs=placed,
        out_specs=(
            P(None, "gx", "gy", "gz", None),
            P(None, "gx", "gy", "gz", None),
            P("gx", "gy", "gz"),
        ),
        check_vma=False,
    )
```

time: 655 us -> 300 us (0.46)
  Pallas kernels: 0 us -> 242 us
  other arithmetic: 254 us -> 27.2 us
  starting transfers between devices: 126 us -> 0 us
  local copies, waits for them, and re-layouts: 126 us -> 18.4 us
  blocking collectives: 79.8 us -> 0 us
  matrix products: 28.6 us -> 0.37 us
  waiting for transfers between devices: 20.6 us -> 0 us
    pallas_call x0 -> x12, Pallas kernels: none -> 242 us  [the longest x2 88.9 us: on_device(): pl.pallas_call(functools.partial(force_kernel, dims), out_shape=jax.Shape...]
    ppermute x48 -> x0, starting transfers between devices: 126 us -> none  [the longest x24 70.9 us: padded(): lax.ppermute(tail, axis, [(i, (i + 1) % count) for i in range(ends)])]
    reduce_sum x221 -> x9, other arithmetic: 132 us -> 7.35 us  [the longest x2 3.08 us: on_device(): jnp.sum(evolved * evolved)]
    mul x242 -> x1, other arithmetic: 95.7 us -> 0.01 us  [active_lists(): offsets = sides * jnp.array(dims, jnp.float32)[None, :]]
    psum x2 -> x0, blocking collectives: 79.8 us -> none  [correlate(): lax.psum((jnp.sum(evolved * evolved), jnp.sum(evolved * exp_map), jnp.sum...]
    dynamic_slice x162 -> x0, local copies, waits for them, and re-layouts: 63.8 us -> none  [the longest x108 63.1 us: born_radius(): lax.scan(born_visit, jnp.zeros((slot_count,), jnp.float32), (blocks, offs...]
    scatter-add x50 -> x0, local copies, waits for them, and re-layouts: 54 us -> none  [splat_window(): density = density.at[low_x + reach:high_x + reach, low_y + reach:high_y +...]
    dot_general x56 -> x2, matrix products: 28.6 us -> 0.37 us  [active_lists(): jnp.dot(keep.astype(jnp.bfloat16), before, preferred_element_type=jnp.flo...]
  transfers between devices with their start and end apart: 48 -> 0, of which waited for: 13 -> 0; matrix products, arithmetic and copies ran while one was open for 48% -> 0% of each run, Pallas kernels for 0% -> 0%
where the time goes in v1:
time: 300 us; the launch traced here: 294 us
  Pallas kernels  242 us (81%)
  other arithmetic  27.2 us (9%)
  local copies, waits for them, and re-layouts  18.4 us (6%)
  between operations  5.66 us (2%)
    pallas_call x2, Pallas kernels, on_device(): pl.pallas_call(functools.partial(force_kernel, dims), out_shape=jax.Shape...  88.9 us
    pallas_call x2, Pallas kernels, on_device(): pl.pallas_call(functools.partial(born_kernel, dims), out_shape=jax.ShapeD...  67.8 us
    pallas_call x2, Pallas kernels, on_device(): pl.pallas_call(functools.partial(evolved_kernel, dims, sizes), out_shape=...  42.2 us
    pallas_call x4, Pallas kernels, exchange(): pl.pallas_call(functools.partial(exchange_kernel, sizes, count, everyone)...  38.1 us

profile of v1, /device:TPU:20, one launch (start us, length us, event | category | flops | bytes accessed | tf_op | source)
XLA Modules:
  0.0 293.8 jit_solution(15461692605532092963)
XLA Ops:
  4.9 1.6 reshape.380.refs_1_
  6.5 12.4 %exchange0.1 = (f32[27,8,512]{2,1,0:T(8,128)}, f32[27,32,128]{2,1,0:T(8,128)}) custom-call(f32[8,512]{1,0:T(8,128)} %concatenate.61.refs_0_.own_ref, f32[32,128]{1,0:T(8,128)} %reshape.380.refs_1_), custom_call_target="tpu_custom_call" | custom-call | tf_op jit(solution)/shard_map/exchange0/pallas_call | solution.py:180
  18.9 1.6 copy.61.own_ref
  20.4 1.1 slice_compare_fusion.1
  21.8 1.2 broadcast_select_fusion.3
  24.7 0.9 select_reduce_fusion.1.list_ref
  26.3 33.9 %born.2.radius_ref = f32[512,1]{1,0:T(8,128)} custom-call(f32[27,8,512]{2,1,0:T(8,128)} %get-tuple-element.9.near_ref, f32[512,8]{1,0:T(8,128)} %copy.61.own_ref, s32[8,108]{1,0:T(8,128)} %select_reduce_fusion.1.list_ref, s32[1,8]{1,0:T(1,128)} %bitcast.148), custom_call_target="tpu_custom_call" | custom-call | tf_op jit(solution)/shard_map/born/pallas_call | solution.py:505
  60.2 1.7 reduce.2
  62.5 21.1 %evolve.2 = f32[26,32,32]{2,1,0:T(8,128)} custom-call(f32[27,8,512]{2,1,0:T(8,128)} %get-tuple-element.9.near_ref, s32[1,3]{1,0:T(1,128)} %add_bitcast_fusion.place_ref), custom_call_target="tpu_custom_call" | custom-call | tf_op jit(solution)/shard_map/evolve/pallas_call | solution.py:512
  83.6 1.7 multiply_reduce_fusion.4
  85.3 2.6 compare_select_fusion.4.refs_1_
  87.9 8.9 %exchange2.2 = (f32[27,1,512]{2,1,0:T(1,128)}, f32[32,1,128]{2,1,0:T(1,128)}) custom-call(f32[1,512]{1,0:T(1,128)} %bitcast.144, f32[1,128]{1,0:T(1,128)} %compare_select_fusion.4.refs_1_), custom_call_target="tpu_custom_call" | custom-call | tf_op jit(solution)/shard_map/exchange2/pallas_call | solution.py:180
  96.8 44.5 %pair.2 = f32[512,3]{1,0:T(8,128)} custom-call(f32[27,8,512]{2,1,0:T(8,128)} %get-tuple-element.9.near_ref, f32[27,1,512]{2,1,0:T(1,128)} %get-tuple-element.10.radii_ref, f32[512,8]{1,0:T(8,128)} %copy.61.own_ref, f32[512,1]{1,0:T(8,128)} %born.2.radius_ref, s32[8,108]{1,0:T(8,128)} %select_reduce_fusion.1.list_ref, s32[1,8]{1,0:T(1,128)} %bitcast.149), custom_call_target="tpu_custom_call" | custom-call | tf_op jit(solution)/shard_map/pair/pallas_call | solution.py:560
  141.3 1.7 copy.63
  146.3 2.0 reshape.385
  149.9 0.9 pad_maximum_fusion.16.sens_ref
  150.8 2.6 fit.2
  154.8 7.9 %exchange1.1.near_ref = f32[27,8,512]{2,1,0:T(8,128)} custom-call(f32[8,512]{1,0:T(8,128)} %concatenate.76.refs_0_.own_ref), custom_call_target="tpu_custom_call" | custom-call | tf_op jit(solution)/shard_map/exchange1/pallas_call | solution.py:180
  162.7 21.1 %evolve.3 = f32[26,32,32]{2,1,0:T(8,128)} custom-call(f32[27,8,512]{2,1,0:T(8,128)} %exchange1.1.near_ref, s32[1,3]{1,0:T(1,128)} %add_bitcast_fusion.place_ref), custom_call_target="tpu_custom_call" | custom-call | tf_op jit(solution)/shard_map/evolve/pallas_call | solution.py:512
  183.8 1.6 copy.70.own_ref
  185.4 1.1 slice_compare_fusion
  186.5 1.2 broadcast_select_fusion.2
  189.5 0.9 select_reduce_fusion.list_ref
  191.1 33.9 %born.3.radius_ref = f32[512,1]{1,0:T(8,128)} custom-call(f32[27,8,512]{2,1,0:T(8,128)} %exchange1.1.near_ref, f32[512,8]{1,0:T(8,128)} %copy.70.own_ref, s32[8,108]{1,0:T(8,128)} %select_reduce_fusion.list_ref, s32[1,8]{1,0:T(1,128)} %bitcast.146), custom_call_target="tpu_custom_call" | custom-call | tf_op jit(solution)/shard_map/born/pallas_call | solution.py:505
  225.0 1.7 reduce.5
  226.7 1.4 multiply_reduce_fusion.1
  228.1 2.4 compare_select_fusion.3.refs_1_
  230.5 8.9 %exchange2.3 = (f32[27,1,512]{2,1,0:T(1,128)}, f32[32,1,128]{2,1,0:T(1,128)}) custom-call(f32[1,512]{1,0:T(1,128)} %bitcast.145, f32[1,128]{1,0:T(1,128)} %compare_select_fusion.3.refs_1_), custom_call_target="tpu_custom_call" | custom-call | tf_op jit(solution)/shard_map/exchange2/pallas_call | solution.py:180
  242.9 0.9 pad_maximum_fusion.17.sens_ref
  243.8 2.6 fit.3
  246.4 44.4 %pair.3 = f32[512,3]{1,0:T(8,128)} custom-call(f32[27,8,512]{2,1,0:T(8,128)} %exchange1.1.near_ref, f32[27,1,512]{2,1,0:T(1,128)} %get-tuple-element.13.radii_ref, f32[512,8]{1,0:T(8,128)} %copy.70.own_ref, f32[512,1]{1,0:T(8,128)} %born.3.radius_ref, s32[8,108]{1,0:T(8,128)} %select_reduce_fusion.list_ref, s32[1,8]{1,0:T(1,128)} %bitcast.147), custom_call_target="tpu_custom_call" | custom-call | tf_op jit(solution)/shard_map/pair/pallas_call | solution.py:560
  290.8 1.1 copy.72
  (108 shorter events, 16.9 us)
Async XLA Ops:
  0.6 83.0 %copy-start.2 = (f32[16,16,16]{2,1,0:T(8,128)S(1)}, f32[16,16,16]{2,1,0:T(8,128)}, u32[]{:S(2)}) copy-start(f32[16,16,16]{2,1,0:T(8,128)} %param.13) | copy-start | bytes 49156
  4.2 17.5 %copy-start.6 = (f32[1,512]{1,0:T(1,128)}, f32[1,512]{1,0:T(1,128)S(1)}, u32[]{:S(2)}) copy-start(f32[1,512]{1,0:T(1,128)S(1)} %get-tuple-element.76) | copy-start | bytes 6148
  4.2 17.5 %copy-start.8 = (f32[1,512]{1,0:T(1,128)}, f32[1,512]{1,0:T(1,128)S(1)}, u32[]{:S(2)}) copy-start(f32[1,512]{1,0:T(1,128)S(1)} %get-tuple-element.77) | copy-start | bytes 6148
  4.2 17.5 %copy-start.10 = (f32[1,512]{1,0:T(1,128)}, f32[1,512]{1,0:T(1,128)S(1)}, u32[]{:S(2)}) copy-start(f32[1,512]{1,0:T(1,128)S(1)} %get-tuple-element.78) | copy-start | bytes 6148
  4.2 17.5 %copy-start.12 = (f32[1,512]{1,0:T(1,128)}, f32[1,512]{1,0:T(1,128)S(1)}, u32[]{:S(2)}) copy-start(f32[1,512]{1,0:T(1,128)S(1)} %get-tuple-element.89) | copy-start | bytes 6148
  4.2 17.4 %copy-start.14 = (f32[1,512]{1,0:T(1,128)}, f32[1,512]{1,0:T(1,128)S(1)}, u32[]{:S(2)}) copy-start(f32[1,512]{1,0:T(1,128)S(1)} %fusion.17) | copy-start | bytes 6148
  148.3 1.3 copy-start.1
  149.3 4.2 %copy-start.4 = (f32[3,1,1,1,512]{4,3,2,1,0:T(1,128)S(1)}, f32[3,1,1,1,512]{4,3,2,1,0:T(1,128)}, u32[]{:S(2)}) copy-start(f32[3,1,1,1,512]{4,3,2,1,0:T(1,128)} %param.8) | copy-start | bytes 18436
  149.3 4.2 %copy-start.5 = (f32[512,3]{0,1:T(4,128)S(1)}, f32[512,3]{0,1:T(4,128)}, u32[]{:S(2)}) copy-start(f32[512,3]{0,1:T(4,128)} %copy.63) | copy-start | bytes 18436
  149.3 4.9 %copy-start.7 = (f32[1,512]{1,0:T(1,128)S(1)}, f32[1,512]{1,0:T(1,128)}, u32[]{:S(2)}) copy-start(f32[1,512]{1,0:T(1,128)} %copy-done.6) | copy-start | bytes 6148
  149.3 4.9 %copy-start.9 = (f32[1,512]{1,0:T(1,128)S(1)}, f32[1,512]{1,0:T(1,128)}, u32[]{:S(2)}) copy-start(f32[1,512]{1,0:T(1,128)} %copy-done.8) | copy-start | bytes 6148
  149.3 4.9 %copy-start.11 = (f32[1,512]{1,0:T(1,128)S(1)}, f32[1,512]{1,0:T(1,128)}, u32[]{:S(2)}) copy-start(f32[1,512]{1,0:T(1,128)} %copy-done.10) | copy-start | bytes 6148
  149.3 4.9 %copy-start.13 = (f32[1,512]{1,0:T(1,128)S(1)}, f32[1,512]{1,0:T(1,128)}, u32[]{:S(2)}) copy-start(f32[1,512]{1,0:T(1,128)} %copy-done.12) | copy-start | bytes 6148
  149.3 4.9 %copy-start.15 = (f32[1,512]{1,0:T(1,128)S(1)}, f32[1,512]{1,0:T(1,128)}, u32[]{:S(2)}) copy-start(f32[1,512]{1,0:T(1,128)} %copy-done.14) | copy-start | bytes 6148
  149.9 76.7 %copy-start.3 = (f32[16,16,16]{2,1,0:T(8,128)S(1)}, f32[16,16,16]{2,1,0:T(8,128)}, u32[]{:S(2)}) copy-start(f32[16,16,16]{2,1,0:T(8,128)} %param.13) | copy-start | bytes 49156
  183.8 42.9 %copy-start = (f32[26,32,32]{2,1,0:T(8,128)S(1)}, f32[26,32,32]{2,1,0:T(8,128)}, u32[]{:S(2)}) copy-start(f32[26,32,32]{2,1,0:T(8,128)} %evolve.3) | copy-start | bytes 319492

commit v2 on v1

--- a/solution.py
+++ b/solution.py
@@ -221,9 +221,41 @@
     return wide, jnp.where(reach, spread(gap * plain), 0.0)
 
 
-def born_kernel(dims, near_ref, own_ref, list_ref, count_ref, out_ref):
-    slots = near_ref.shape[-1]
-    pieces = slots // LANES
+def sort_kernel(own_ref, chunk_ref, column_ref, row_ref, rank_ref):
+    slots = own_ref.shape[-1]
+    own = own_ref[...]
+    turned = own.T
+    first = lax.broadcasted_iota(jnp.int32, (slots, slots), 0)
+    second = lax.broadcasted_iota(jnp.int32, (slots, slots), 1)
+    earlier = second < first
+    far = 9.0e3
+    part_row = jnp.zeros((1, slots), jnp.float32)
+    part_column = jnp.zeros((slots, 1), jnp.float32)
+    for axis, size in ((0, slots // 2), (1, LANES), (2, 1)):
+        row = jnp.where(own[7:8, :] > 0.5, jnp.clip(own[axis : axis + 1, :], -5.0e3, 5.0e3), far)
+        column = jnp.where(
+            turned[:, 7:8] > 0.5, jnp.clip(turned[:, axis : axis + 1], -5.0e3, 5.0e3), far
+        )
+        row = row + 1.0e5 * part_row
+        column = column + 1.0e5 * part_column
+        before = jnp.where((row < column) | ((row == column) & earlier), 1.0, 0.0)
+        rank_column = jnp.sum(before, axis=1, keepdims=True)
+        rank_row = float(slots - 1) - jnp.sum(before, axis=0, keepdims=True)
+        part_column = jnp.floor(rank_column * (1.0 / size))
+        part_row = jnp.floor(rank_row * (1.0 / size))
+    place = jnp.where(rank_column.astype(jnp.int32) == second, 1.0, 0.0)
+    ordered = jnp.dot(
+        own, place, precision=lax.Precision.HIGHEST, preferred_element_type=jnp.float32
+    )
+    row_ref[...] = ordered
+    column_ref[...] = ordered.T
+    for k in range(slots // LANES):
+        chunk_ref[k] = ordered[:, k * LANES : (k + 1) * LANES]
+    rank_ref[...] = rank_row.astype(jnp.int32)
+
+
+def born_kernel(near_ref, own_ref, list_ref, count_ref, offset_ref, out_ref):
+    slots = own_ref.shape[0]
 
     def block(index, carry):
         base = pl.multiple_of(index * ROWS, ROWS)
@@ -234,17 +266,13 @@
 
         def visit(step, summed):
             number = list_ref[index, step]
-            cell = number // pieces
-            lane = pl.multiple_of(number % pieces * LANES, LANES)
-            sides = sides_of(cell)
             squared = None
             for axis in range(3):
-                row = near_ref[cell, axis : axis + 1, pl.ds(lane, LANES)]
-                shift = sides[axis].astype(jnp.float32) * float(dims[axis])
-                gap = own[axis] - (row + shift)
+                row = near_ref[number, axis : axis + 1, :] + offset_ref[number, axis]
+                gap = own[axis] - row
                 squared = gap * gap if squared is None else squared + gap * gap
             smooth = jnp.maximum(1.0 - squared * (1.0 / (CUTOFF * CUTOFF)), 0.0)
-            weight = near_ref[cell, 4:5, pl.ds(lane, LANES)]
+            weight = near_ref[number, 4:5, :]
             return summed + jnp.exp(squared * -0.125) * (smooth * smooth) * weight
 
         summed = lax.fori_loop(
@@ -260,9 +288,12 @@
     lax.fori_loop(0, slots // ROWS, block, 0)
 
 
-def force_kernel(dims, near_ref, radii_ref, own_ref, radius_ref, list_ref, count_ref, out_ref):
-    slots = near_ref.shape[-1]
-    pieces = slots // LANES
+def force_kernel(
+    scale, near_ref, radii_ref, own_ref, radius_ref, fit_ref, rank_ref, list_ref, count_ref,
+    offset_ref, out_ref, held_ref,
+):
+    slots = own_ref.shape[0]
+    held_ref[...] = jnp.zeros_like(held_ref)
 
     def block(index, carry):
         base = pl.multiple_of(index * ROWS, ROWS)
@@ -275,28 +306,21 @@
 
         def visit(step, summed):
             number = list_ref[index, step]
-            cell = number // pieces
-            lane = pl.multiple_of(number % pieces * LANES, LANES)
-            sides = sides_of(cell)
             squared = None
             gaps = []
             for axis in range(3):
-                row = near_ref[cell, axis : axis + 1, pl.ds(lane, LANES)]
-                shift = sides[axis].astype(jnp.float32) * float(dims[axis])
-                gap = own[axis] - (row + shift)
+                row = near_ref[number, axis : axis + 1, :] + offset_ref[number, axis]
+                gap = own[axis] - row
                 gaps.append(gap)
                 squared = gap * gap if squared is None else squared + gap * gap
             smooth = jnp.maximum(1.0 - squared * (1.0 / (CUTOFF * CUTOFF)), 0.0)
-            near_radius = radii_ref[cell, :, pl.ds(lane, LANES)]
-            charge = near_ref[cell, 3:4, pl.ds(lane, LANES)]
+            near_radius = radii_ref[number]
+            charge = near_ref[number, 3:4, :]
             fading = jnp.exp(squared * (inverse_radius * (1.0 / near_radius)))
             inverse = lax.rsqrt(squared + (radius * near_radius) * fading)
-            common = (
-                (charge * (smooth * inverse))
-                * (
-                    2.0 / (CUTOFF * CUTOFF)
-                    + (smooth * (inverse * inverse)) * (0.5 - 0.125 * fading)
-                )
+            common = (charge * (smooth * inverse)) * (
+                2.0 / (CUTOFF * CUTOFF)
+                + (smooth * (inverse * inverse)) * (0.5 - 0.125 * fading)
             )
             return tuple(total + common * gap for total, gap in zip(summed, gaps))
 
@@ -304,12 +328,18 @@
         summed = lax.fori_loop(0, count_ref[0, index], visit, (zero, zero, zero))
         charge = own_ref[pl.ds(base, ROWS), 3:4]
         for axis in range(3):
-            out_ref[pl.ds(base, ROWS), axis : axis + 1] = -charge * jnp.sum(
+            held_ref[pl.ds(base, ROWS), axis : axis + 1] = -charge * jnp.sum(
                 summed[axis], axis=1, keepdims=True
             )
         return carry
 
     lax.fori_loop(0, slots // ROWS, block, 0)
+    force = held_ref[...].T + scale * fit_ref[...]
+    slot = lax.broadcasted_iota(jnp.int32, (slots, slots), 0)
+    back = jnp.where(slot == rank_ref[...], 1.0, 0.0)
+    out_ref[...] = jnp.dot(
+        force, back, precision=lax.Precision.HIGHEST, preferred_element_type=jnp.float32
+    )
 
 
 def halves(value):
@@ -317,65 +347,104 @@
     return high, (value - high.astype(jnp.float32)).astype(jnp.bfloat16)
 
 
-def evolved_kernel(dims, sizes, near_ref, place_ref, out_ref, px_ref, py_ref, pz_ref, total_ref):
+def evolved_kernel(
+    dims, sizes, near_ref, map_ref, place_ref, out_ref, part_ref, px_ref, py_ref, pz_ref, total_ref
+):
     places = [place_ref[0, k] for k in range(3)]
-    depth = dims[2] + 2 * PAD
+    pieces = near_ref.shape[0] // 27
+    depth = dims[2]
+
+    def there(sides):
+        inside = None
+        for axis in range(3):
+            spot = places[axis] + sides[axis]
+            good = (spot >= 0) & (spot < sizes[axis])
+            inside = good if inside is None else inside & good
+        return inside
 
     def profiles(cell, carry):
         sides = sides_of(cell)
-        made = [
-            profile_rows(
-                near_ref[cell, axis : axis + 1, :],
-                sides[axis],
-                dims[axis],
-                places[axis],
-                sizes[axis],
-                False,
-            )
-            for axis in range(3)
-        ]
-        px_ref[cell] = made[0] * near_ref[cell, 5:6, :]
-        py_ref[cell] = made[1]
-        high, low = halves(made[2])
-        pz_ref[cell, 0:depth, :] = high
-        pz_ref[cell, depth : 2 * depth, :] = low
+
+        @pl.when(there(sides))
+        def _():
+            for piece in range(pieces):
+                atoms = near_ref.at[cell * pieces + piece]
+                lanes = slice(piece * LANES, (piece + 1) * LANES)
+                made = [
+                    profile_rows(
+                        atoms[axis : axis + 1, :],
+                        sides[axis],
+                        dims[axis],
+                        places[axis],
+                        sizes[axis],
+                        False,
+                    )[PAD : PAD + dims[axis]]
+                    for axis in range(3)
+                ]
+                px_ref[cell, :, lanes] = made[0] * atoms[5:6, :]
+                py_ref[cell, :, lanes] = made[1]
+                high, low = halves(made[2])
+                pz_ref[cell, 0:depth, lanes] = high
+                pz_ref[cell, depth : 2 * depth, lanes] = low
+
         return carry
 
     lax.fori_loop(0, 27, profiles, 0)
-    half_x = dims[0] // 2 + REACH
-    half_y = dims[1] // 2 + PAD
-    rows = half_x * half_y
-    for hx in range(2):
-        first = PAD - REACH if hx == 0 else PAD + dims[0] // 2
-        for hy in range(2):
-            total_ref[...] = jnp.zeros_like(total_ref)
-
-            def add(step, carry):
-                cell = (hx + step // 6) * 9 + (hy + step // 3 % 2) * 3 + step % 3
-                py = py_ref[cell, hy * half_y : (hy + 1) * half_y, :]
-                pieces_high, pieces_low = [], []
-                for k in range(half_x):
-                    high, low = halves(px_ref[cell, first + k : first + k + 1, :] * py)
-                    pieces_high.append(high)
-                    pieces_low.append(low)
-                plane = jnp.concatenate(pieces_high + pieces_low, axis=0)
-                total_ref[...] += lax.dot_general(
-                    plane,
-                    pz_ref[cell],
-                    (((1,), (1,)), ((), ())),
-                    preferred_element_type=jnp.float32,
+    out_ref[...] = jnp.zeros_like(out_ref)
+    spans_x = ((0, REACH), (0, dims[0]), (dims[0] - REACH, dims[0]))
+    spans_y = ((0, PAD), (0, dims[1]), (dims[1] - PAD, dims[1]))
+    for ix in range(3):
+        for iy in range(3):
+            x0, x1 = spans_x[ix]
+            y0, y1 = spans_y[iy]
+            rows = (x1 - x0) * (y1 - y0)
+
+            @pl.when(there((ix - 1, iy - 1, 0)))
+            def _(ix=ix, iy=iy, x0=x0, x1=x1, y0=y0, y1=y1, rows=rows):
+                total_ref[0 : 2 * rows, :] = jnp.zeros((2 * rows, 2 * depth), jnp.float32)
+
+                def add(iz, carry):
+                    cell = ix * 9 + iy * 3 + iz
+
+                    @pl.when(there((ix - 1, iy - 1, iz - 1)))
+                    def _():
+                        py = py_ref[cell, y0:y1, :]
+                        pieces_high, pieces_low = [], []
+                        for k in range(x0, x1):
+                            value = px_ref[cell, k : k + 1, :] * py
+                            upper = value.astype(jnp.bfloat16).astype(jnp.float32)
+                            pieces_high.append(upper)
+                            pieces_low.append(value - upper)
+                        plane = jnp.concatenate(pieces_high + pieces_low, axis=0)
+                        total_ref[0 : 2 * rows, :] += lax.dot_general(
+                            plane.astype(jnp.bfloat16),
+                            pz_ref[cell],
+                            (((1,), (1,)), ((), ())),
+                            preferred_element_type=jnp.float32,
+                        )
+
+                    return carry
+
+                lax.fori_loop(0, 3, add, 0)
+                result = (
+                    total_ref[0:rows, 0:depth]
+                    + total_ref[0:rows, depth : 2 * depth]
+                    + total_ref[rows : 2 * rows, 0:depth]
                 )
-                return carry
-
-            lax.fori_loop(0, 12, add, 0)
-            result = (
-                total_ref[0:rows, 0:depth]
-                + total_ref[0:rows, depth : 2 * depth]
-                + total_ref[rows : 2 * rows, 0:depth]
-            )
-            out_ref[
-                hx * half_x : (hx + 1) * half_x, hy * half_y : (hy + 1) * half_y, :
-            ] = result.reshape(half_x, half_y, depth)
+                out_ref[x0:x1, y0:y1, :] += result.reshape(x1 - x0, y1 - y0, depth)
+
+    evolved = out_ref[...]
+    given = map_ref[...]
+    lane = lax.broadcasted_iota(jnp.int32, (1, LANES), 1)
+    part_ref[...] = jnp.where(
+        lane == 0,
+        jnp.sum(evolved * evolved),
+        jnp.where(
+            lane == 1,
+            jnp.sum(evolved * given),
+            jnp.where(lane == 2, jnp.sum(given * given), 0.0),
+        ),
+    )
 
 
 def fit_kernel(dims, sizes, own_ref, place_ref, sens_ref, out_ref, big_ref):
@@ -407,6 +476,7 @@
         force[1] = force[1] + here * turned_y
         force[2] = force[2] + here * turned_z
     mass = own_ref[5:6, :]
+    out_ref[...] = jnp.zeros_like(out_ref)
     for axis in range(3):
         out_ref[axis : axis + 1, :] = mass * force[axis]
 
@@ -432,28 +502,24 @@
     )
 
 
-def active_lists(near, dims):
-    slots = near.shape[-1]
-    pieces = slots // LANES
+def active_lists(near, columns, offsets):
+    whole = near.shape[0]
+    slots = columns.shape[0]
     blocks = slots // ROWS
-    number = jnp.arange(27, dtype=jnp.int32)
-    sides = jnp.stack(sides_of(number), axis=1).astype(jnp.float32)
-    offsets = sides * jnp.array(dims, jnp.float32)[None, :]
     coords = near[:, 0:3, :] + offsets[:, :, None]
     live = near[:, 7:8, :] > 0.5
     big = 1e30
-    low = jnp.where(live, coords, big).reshape(27, 3, pieces, LANES).min(axis=-1)
-    high = jnp.where(live, coords, -big).reshape(27, 3, pieces, LANES).max(axis=-1)
-    own_low = jnp.where(live[13], coords[13], big).reshape(3, blocks, ROWS).min(axis=-1)
-    own_high = jnp.where(live[13], coords[13], -big).reshape(3, blocks, ROWS).max(axis=-1)
+    low = jnp.where(live, coords, big).min(axis=-1)
+    high = jnp.where(live, coords, -big).max(axis=-1)
+    grouped = columns.reshape(blocks, ROWS, columns.shape[1])
+    own_live = grouped[:, :, 7:8] > 0.5
+    own_low = jnp.where(own_live, grouped[:, :, 0:3], big).min(axis=1)
+    own_high = jnp.where(own_live, grouped[:, :, 0:3], -big).max(axis=1)
     apart = jnp.maximum(
-        low[:, :, :, None] - own_high[None, :, None, :],
-        own_low[None, :, None, :] - high[:, :, :, None],
+        low[None, :, :] - own_high[:, None, :], own_low[:, None, :] - high[None, :, :]
     )
     apart = jnp.maximum(apart, 0.0)
-    keep = jnp.sum(apart * apart, axis=1) < CUTOFF * CUTOFF * 1.001
-    keep = keep.reshape(27 * pieces, blocks).T
-    whole = 27 * pieces
+    keep = jnp.sum(apart * apart, axis=-1) < CUTOFF * CUTOFF * 1.001
     index = jnp.arange(whole, dtype=jnp.int32)
     before = (index[:, None] <= index[None, :]).astype(jnp.bfloat16)
     spot = jnp.dot(
@@ -491,55 +557,61 @@
         axis=0,
     )
     current = start
-    target = jnp.sum(exp_map * exp_map)
+    pieces = slots // LANES
+    number = jnp.arange(27 * pieces, dtype=jnp.int32) // pieces
+    offsets = jnp.stack(sides_of(number), axis=1).astype(jnp.float32) * jnp.array(
+        dims, jnp.float32
+    )
     framed = None
     for step in range(STEPS):
         own = jnp.concatenate([current, fixed], axis=0)
+        chunks, columns, ordered, rank = pl.pallas_call(
+            sort_kernel,
+            out_shape=[
+                jax.ShapeDtypeStruct((pieces, 8, LANES), jnp.float32),
+                jax.ShapeDtypeStruct((slots, 8), jnp.float32),
+                jax.ShapeDtypeStruct((8, slots), jnp.float32),
+                jax.ShapeDtypeStruct((1, slots), jnp.int32),
+            ],
+            in_specs=[VMEM],
+            out_specs=[VMEM] * 4,
+            name="sort",
+        )(own)
         if step == 0:
-            near, bricks = exchange([own, exp_map.reshape(-1, LANES)], None, 0)
+            near, bricks = exchange([chunks, exp_map.reshape(-1, LANES)], None, 0)
             framed = frame_map(bricks, dims)
         else:
-            (near,) = exchange([own], None, 1)
-        columns = own.T
-        lists, counts = active_lists(near, dims)
+            (near,) = exchange([chunks], None, 1)
+        near = near.reshape(27 * pieces, 8, LANES)
+        lists, counts = active_lists(near, columns, offsets)
         radius = pl.pallas_call(
-            functools.partial(born_kernel, dims),
+            born_kernel,
             out_shape=jax.ShapeDtypeStruct((slots, 1), jnp.float32),
-            in_specs=[VMEM, VMEM, SMEM, SMEM],
+            in_specs=[VMEM, VMEM, SMEM, SMEM, SMEM],
             out_specs=VMEM,
             name="born",
-        )(near, columns, lists, counts)
-        wide = pl.pallas_call(
+        )(near, columns, lists, counts, offsets)
+        evolved, part = pl.pallas_call(
             functools.partial(evolved_kernel, dims, sizes),
-            out_shape=jax.ShapeDtypeStruct(
-                (dims[0] + 2 * REACH, dims[1] + 2 * PAD, dims[2] + 2 * PAD), jnp.float32
-            ),
-            in_specs=[VMEM, SMEM],
-            out_specs=VMEM,
+            out_shape=[
+                jax.ShapeDtypeStruct(dims, jnp.float32),
+                jax.ShapeDtypeStruct((1, LANES), jnp.float32),
+            ],
+            in_specs=[VMEM, VMEM, SMEM],
+            out_specs=[VMEM, VMEM],
             scratch_shapes=[
-                pltpu.VMEM((27, dims[0] + 2 * PAD, slots), jnp.float32),
-                pltpu.VMEM((27, dims[1] + 2 * PAD, slots), jnp.float32),
-                pltpu.VMEM((27, 2 * (dims[2] + 2 * PAD), slots), jnp.bfloat16),
-                pltpu.VMEM(
-                    (
-                        2 * (dims[0] // 2 + REACH) * (dims[1] // 2 + PAD),
-                        2 * (dims[2] + 2 * PAD),
-                    ),
-                    jnp.float32,
-                ),
+                pltpu.VMEM((27, dims[0], slots), jnp.float32),
+                pltpu.VMEM((27, dims[1], slots), jnp.float32),
+                pltpu.VMEM((27, 2 * dims[2], slots), jnp.bfloat16),
+                pltpu.VMEM((2 * dims[0] * dims[1], 2 * dims[2]), jnp.float32),
             ],
             name="evolve",
-        )(near, place)
-        evolved = wide[
-            REACH : REACH + dims[0], PAD : PAD + dims[1], PAD : PAD + dims[2]
-        ]
-        lane = lax.broadcasted_iota(jnp.int32, (1, LANES), 1)
-        part = jnp.where(
-            lane == 0,
-            jnp.sum(evolved * evolved),
-            jnp.where(lane == 1, jnp.sum(evolved * exp_map), jnp.where(lane == 2, target, 0.0)),
-        )
-        near_radius, parts = exchange([radius.reshape(1, slots)], part, 2)
+        )(near, exp_map, place)
+        near_radius, halo, parts = exchange(
+            [radius.reshape(pieces, 1, LANES), evolved.reshape(-1, LANES)], part, 2
+        )
+        near_radius = near_radius.reshape(27 * pieces, 1, LANES)
+        wide = frame_map(halo, dims)
         sums = jnp.sum(parts, axis=(0, 1))
         squares, cross_sum, whole_target = sums[0], sums[1], sums[2]
         norm = jnp.sqrt((squares + EPSILON) * (whole_target + EPSILON))
@@ -551,20 +623,20 @@
         stacked = jnp.concatenate([high, high, low], axis=1)
         fit = pl.pallas_call(
             functools.partial(fit_kernel, dims, sizes),
-            out_shape=jax.ShapeDtypeStruct((3, slots), jnp.float32),
+            out_shape=jax.ShapeDtypeStruct((8, slots), jnp.float32),
             in_specs=[VMEM, SMEM, VMEM],
             out_specs=VMEM,
             scratch_shapes=[pltpu.VMEM((stacked.shape[0], 2 * slots), jnp.float32)],
             name="fit",
-        )(own, place, stacked)
-        pair = pl.pallas_call(
-            functools.partial(force_kernel, dims),
-            out_shape=jax.ShapeDtypeStruct((slots, 3), jnp.float32),
-            in_specs=[VMEM, VMEM, VMEM, VMEM, SMEM, SMEM],
+        )(ordered, place, stacked)
+        force = pl.pallas_call(
+            functools.partial(force_kernel, scale),
+            out_shape=jax.ShapeDtypeStruct((8, slots), jnp.float32),
+            in_specs=[VMEM] * 6 + [SMEM] * 3,
             out_specs=VMEM,
+            scratch_shapes=[pltpu.VMEM((slots, 8), jnp.float32)],
             name="pair",
-        )(near, near_radius, columns, radius, lists, counts)
-        force = pair.T + scale * fit
+        )(near, near_radius, columns, radius, fit, rank, lists, counts, offsets)[0:3]
         current = current + STEP_SIZE * (living * force)
     shape = positions.shape
     return ((current - start).reshape(shape), force.reshape(shape), evolved)

time: 300 us -> 209 us (0.70)
  Pallas kernels: 242 us -> 144 us
  local copies, waits for them, and re-layouts: 18.4 us -> 32.2 us
  other arithmetic: 27.2 us -> 22.2 us
    pallas_call x4 -> x6, Pallas kernels: 157 us -> 75.3 us  [the longest x2 35.8 us: on_device(): pl.pallas_call(functools.partial(force_kernel, scale), out_shape=jax.Shap...]
    pallas_call x2, Pallas kernels: 42.2 us -> 18.5 us  [on_device(): pl.pallas_call(functools.partial(evolved_kernel, dims, sizes), out_shape=...]
    slice x9 -> x27, local copies, waits for them, and re-layouts: 0.84 us -> 8.47 us  [join(): lax.slice_in_dim(parts[0], length - reaches[axis], length, axis=axis)]
    select_n x6 -> x0, other arithmetic: 7.52 us -> none  [the longest x2 5 us: on_device(): jnp.where(lane == 0, jnp.sum(evolved * evolved), jnp.where(lane == 1, jnp...]
    pallas_call x4, Pallas kernels: 38.1 us -> 45.1 us  [exchange(): pl.pallas_call(functools.partial(exchange_kernel, sizes, count, everyone)...]
    reshape x1 -> x3, local copies, waits for them, and re-layouts: 2.02 us -> 6.04 us  [frame_map(): cube = bricks.reshape((3, 3, 3) + dims)]
    transpose x2 -> x0, local copies, waits for them, and re-layouts: 3.18 us -> none  [on_device(): columns = own.T]
    reduce_sum x4 -> x2, other arithmetic: 3.25 us -> 0.16 us  [active_lists(): keep = jnp.sum(apart * apart, axis=-1) < CUTOFF * CUTOFF * 1.001]
where the time goes in v2:
time: 209 us; the launch traced here: 205 us
  Pallas kernels  144 us (69%)
  local copies, waits for them, and re-layouts  32.2 us (15%)
  other arithmetic  22.2 us (11%)
  between operations  6.01 us (3%)
    pallas_call x4, Pallas kernels, exchange(): pl.pallas_call(functools.partial(exchange_kernel, sizes, count, everyone)...  45.1 us
    pallas_call x2, Pallas kernels, on_device(): pl.pallas_call(functools.partial(force_kernel, scale), out_shape=jax.Shap...  35.8 us
    pallas_call x2, Pallas kernels, on_device(): pl.pallas_call(born_kernel, out_shape=jax.ShapeDtypeStruct((slots, 1), jn...  25.5 us
    pallas_call x2, Pallas kernels, on_device(): pl.pallas_call(functools.partial(evolved_kernel, dims, sizes), out_shape=...  18.5 us
    pallas_call x2, Pallas kernels, on_device(): pl.pallas_call(sort_kernel, out_shape=[jax.ShapeDtypeStruct((pieces, 8, L...  14.1 us
    slice x27, local copies, waits for them, and re-layouts, join(): lax.slice_in_dim(parts[0], length - reaches[axis], length, axis=axis)  8.47 us
    reshape x3, local copies, waits for them, and re-layouts, frame_map(): cube = bricks.reshape((3, 3, 3) + dims)  6.04 us
    pallas_call x2, Pallas kernels, on_device(): pl.pallas_call(functools.partial(fit_kernel, dims, sizes), out_shape=jax....  5.24 us

profile of v2, /device:TPU:20, one launch (start us, length us, event | category | flops | bytes accessed | tf_op | source)
XLA Modules:
  0.0 204.9 jit_solution(18247729527829651066)
XLA Ops:
  4.8 7.0 %sort.2 = (f32[4,8,128]{2,1,0:T(8,128)}, f32[512,8]{1,0:T(8,128)}, f32[8,512]{1,0:T(8,128)}, s32[1,512]{1,0:T(1,128)}) custom-call(f32[8,512]{1,0:T(8,128)} %concatenate.136.own_ref), custom_call_target="tpu_custom_call" | custom-call | tf_op jit(solution)/shard_map/sort/pallas_call | solution.py:568
  11.8 1.6 reshape.315.refs_1_
  13.4 12.4 %exchange0.1 = (f32[27,4,8,128]{3,2,1,0:T(8,128)}, f32[27,32,128]{2,1,0:T(8,128)}) custom-call(f32[4,8,128]{2,1,0:T(8,128)} %get-tuple-element.23.refs_0_, f32[32,128]{1,0:T(8,128)} %reshape.315.refs_1_), custom_call_target="tpu_custom_call" | custom-call | tf_op jit(solution)/shard_map/exchange0/pallas_call | solution.py:180
  25.9 1.1 slice_compare_fusion.1
  27.2 1.5 select_reduce_fusion.9
  28.9 1.1 slice.727
  30.1 1.1 select_reduce_fusion.5
  33.5 12.6 %born.2.radius_ref = f32[512,1]{1,0:T(8,128)} custom-call(f32[108,8,128]{2,1,0:T(8,128)} %bitcast.259, f32[512,8]{1,0:T(8,128)} %get-tuple-element.25.own_ref, s32[8,108]{1,0:T(8,128)} %select_reduce_fusion.1.list_ref, s32[1,8]{1,0:T(1,128)} %bitcast.300, f32[108,3]{1,0:T(8,128)} %copy-done), custom_call_target="tpu_custom_call" | custom-call | tf_op jit(solution)/shard_map/born/pallas_call | solution.py:587
  46.1 1.7 reduce.1
  48.4 9.1 %evolve.2 = (f32[16,16,16]{2,1,0:T(8,128)}, f32[1,128]{1,0:T(1,128)}) custom-call(f32[108,8,128]{2,1,0:T(8,128)} %bitcast.260, f32[16,16,16]{2,1,0:T(8,128)} %map_ref.3, s32[1,3]{1,0:T(1,128)} %add_bitcast_fusion.place_ref), custom_call_target="tpu_custom_call" | custom-call | tf_op jit(solution)/shard_map/evolve/pallas_call | solution.py:594
  57.5 1.6 reshape.320.refs_1_
  59.1 11.6 %exchange2.2 = (f32[27,4,1,128]{3,2,1,0:T(1,128)}, f32[27,32,128]{2,1,0:T(8,128)}, f32[32,1,128]{2,1,0:T(1,128)}) custom-call(f32[4,1,128]{2,1,0:T(1,128)} %bitcast.298, f32[32,128]{1,0:T(8,128)} %reshape.320.refs_1_, f32[1,128]{1,0:T(1,128)} %get-tuple-element.27.refs_2_), custom_call_target="tpu_custom_call" | custom-call | tf_op jit(solution)/shard_map/exchange2/pallas_call | solution.py:180
  70.7 2.0 reshape.323
  72.8 1.2 slice_bitcast_fusion.41
  85.0 2.0 reshape.322
  89.1 1.4 fusion.19
  91.4 2.6 %fit.2.fit_ref = f32[8,512]{1,0:T(8,128)} custom-call(f32[8,512]{1,0:T(8,128)} %get-tuple-element.29.own_ref, s32[1,3]{1,0:T(1,128)} %add_bitcast_fusion.place_ref, bf16[832,96]{1,0:T(8,128)(2,1)} %pad_maximum_fusion.48.sens_ref), custom_call_target="tpu_custom_call" | custom-call | tf_op jit(solution)/shard_map/fit/pallas_call | solution.py:624
  94.0 17.8 %pair.2 = f32[8,512]{1,0:T(8,128)} custom-call(f32[108,8,128]{2,1,0:T(8,128)} %bitcast.261, f32[108,1,128]{2,1,0:T(1,128)} %bitcast.295, f32[512,8]{1,0:T(8,128)} %get-tuple-element.25.own_ref, f32[512,1]{1,0:T(8,128)} %born.2.radius_ref, f32[8,512]{1,0:T(8,128)} %fit.2.fit_ref, s32[1,512]{1,0:T(1,128)} %get-tuple-element.33.rank_ref, ...), custom_call_target="tpu_custom_call" | custom-call | tf_op jit(solution)/shard_map/pair/pallas_call | solution.py:632
  113.2 7.0 %sort.3 = (f32[4,8,128]{2,1,0:T(8,128)}, f32[512,8]{1,0:T(8,128)}, f32[8,512]{1,0:T(8,128)}, s32[1,512]{1,0:T(1,128)}) custom-call(f32[8,512]{1,0:T(8,128)} %concatenate.164.own_ref), custom_call_target="tpu_custom_call" | custom-call | tf_op jit(solution)/shard_map/sort/pallas_call | solution.py:568
  120.2 1.1 slice.822
  121.4 1.1 select_reduce_fusion.3
  122.7 9.5 %exchange1.1 = f32[27,4,8,128]{3,2,1,0:T(8,128)} custom-call(f32[4,8,128]{2,1,0:T(8,128)} %get-tuple-element.34.refs_0_), custom_call_target="tpu_custom_call" | custom-call | tf_op jit(solution)/shard_map/exchange1/pallas_call | solution.py:180
  132.2 1.1 slice_compare_fusion
  133.3 1.5 select_reduce_fusion.7
  137.1 12.8 %born.3.radius_ref = f32[512,1]{1,0:T(8,128)} custom-call(f32[108,8,128]{2,1,0:T(8,128)} %bitcast.254, f32[512,8]{1,0:T(8,128)} %get-tuple-element.35.own_ref, s32[8,108]{1,0:T(8,128)} %select_reduce_fusion.list_ref, s32[1,8]{1,0:T(1,128)} %bitcast.302, f32[108,3]{1,0:T(8,128)} %copy-done), custom_call_target="tpu_custom_call" | custom-call | tf_op jit(solution)/shard_map/born/pallas_call | solution.py:587
  149.9 1.7 reduce.3
  151.6 9.4 %evolve.3 = (f32[16,16,16]{2,1,0:T(8,128)}, f32[1,128]{1,0:T(1,128)}) custom-call(f32[108,8,128]{2,1,0:T(8,128)} %bitcast.255, f32[16,16,16]{2,1,0:T(8,128)} %map_ref.3, s32[1,3]{1,0:T(1,128)} %add_bitcast_fusion.place_ref), custom_call_target="tpu_custom_call" | custom-call | tf_op jit(solution)/shard_map/evolve/pallas_call | solution.py:594
  161.0 1.6 reshape.327.refs_1_
  162.6 11.7 %exchange2.3 = (f32[27,4,1,128]{3,2,1,0:T(1,128)}, f32[27,32,128]{2,1,0:T(8,128)}, f32[32,1,128]{2,1,0:T(1,128)}) custom-call(f32[4,1,128]{2,1,0:T(1,128)} %bitcast.299, f32[32,128]{1,0:T(8,128)} %reshape.327.refs_1_, f32[1,128]{1,0:T(1,128)} %get-tuple-element.37.refs_2_), custom_call_target="tpu_custom_call" | custom-call | tf_op jit(solution)/shard_map/exchange2/pallas_call | solution.py:180
  177.7 2.0 reshape.329
  182.4 2.6 %fit.3.fit_ref = f32[8,512]{1,0:T(8,128)} custom-call(f32[8,512]{1,0:T(8,128)} %get-tuple-element.39.own_ref, s32[1,3]{1,0:T(1,128)} %add_bitcast_fusion.place_ref, bf16[832,96]{1,0:T(8,128)(2,1)} %pad_maximum_fusion.49.sens_ref), custom_call_target="tpu_custom_call" | custom-call | tf_op jit(solution)/shard_map/fit/pallas_call | solution.py:624
  185.0 18.0 %pair.3 = f32[8,512]{1,0:T(8,128)} custom-call(f32[108,8,128]{2,1,0:T(8,128)} %bitcast.256, f32[108,1,128]{2,1,0:T(1,128)} %bitcast.296, f32[512,8]{1,0:T(8,128)} %get-tuple-element.35.own_ref, f32[512,1]{1,0:T(8,128)} %born.3.radius_ref, f32[8,512]{1,0:T(8,128)} %fit.3.fit_ref, s32[1,512]{1,0:T(1,128)} %get-tuple-element.42.rank_ref, ...), custom_call_target="tpu_custom_call" | custom-call | tf_op jit(solution)/shard_map/pair/pallas_call | solution.py:632
  (167 shorter events, 28.4 us)
Async XLA Ops:
  3.4 23.6 %copy-start.32 = (f32[1,512]{1,0:T(1,128)}, f32[1,512]{1,0:T(1,128)S(1)}, u32[]{:S(2)}) copy-start(f32[1,512]{1,0:T(1,128)S(1)} %get-tuple-element.157) | copy-start | bytes 6148
  3.4 23.6 %copy-start.34 = (f32[1,512]{1,0:T(1,128)}, f32[1,512]{1,0:T(1,128)S(1)}, u32[]{:S(2)}) copy-start(f32[1,512]{1,0:T(1,128)S(1)} %get-tuple-element.168) | copy-start | bytes 6148
  3.5 23.6 %copy-start.36 = (f32[1,512]{1,0:T(1,128)}, f32[1,512]{1,0:T(1,128)S(1)}, u32[]{:S(2)}) copy-start(f32[1,512]{1,0:T(1,128)S(1)} %fusion.36) | copy-start | bytes 6148
  27.2 6.3 %copy-start = (f32[108,3]{1,0:T(8,128)}, f32[108,3]{1,0:T(8,128)S(1)}, u32[]{:S(2)}) copy-start(f32[108,3]{1,0:T(8,128)S(1)} %broadcast_multiply_fusion.offset_ref) | copy-start | bytes 3892
  87.0 1.5 copy-start.3
  87.0 1.5 copy-start.4
  87.0 1.5 copy-start.5
  87.0 1.5 copy-start.6
  87.0 1.5 copy-start.7
  87.0 1.5 copy-start.8
  87.0 1.5 copy-start.9
  87.0 1.5 copy-start.10
  87.0 1.5 copy-start.11
  87.1 1.5 copy-start.19
  87.1 1.5 copy-start.20
  87.2 1.6 copy-start.21
  87.2 1.6 copy-start.22
  87.2 1.6 copy-start.23
  87.2 1.7 copy-start.24
  87.2 1.7 copy-start.25
  87.2 1.7 copy-start.26
  87.2 1.8 copy-start.27
  87.2 1.8 copy-start.28
  87.2 1.8 copy-start.29
  89.0 22.8 %copy-start.31 = (f32[3,1,1,1,512]{4,3,2,1,0:T(1,128)S(1)}, f32[3,1,1,1,512]{4,3,2,1,0:T(1,128)}, u32[]{:S(2)}) copy-start(f32[3,1,1,1,512]{4,3,2,1,0:T(1,128)} %param.7) | copy-start | bytes 18436
  89.0 23.5 %copy-start.33 = (f32[1,512]{1,0:T(1,128)S(1)}, f32[1,512]{1,0:T(1,128)}, u32[]{:S(2)}) copy-start(f32[1,512]{1,0:T(1,128)} %copy-done.32) | copy-start | bytes 6148
  89.0 23.5 %copy-start.35 = (f32[1,512]{1,0:T(1,128)S(1)}, f32[1,512]{1,0:T(1,128)}, u32[]{:S(2)}) copy-start(f32[1,512]{1,0:T(1,128)} %copy-done.34) | copy-start | bytes 6148
  89.1 23.5 %copy-start.37 = (f32[1,512]{1,0:T(1,128)S(1)}, f32[1,512]{1,0:T(1,128)}, u32[]{:S(2)}) copy-start(f32[1,512]{1,0:T(1,128)} %copy-done.36) | copy-start | bytes 6148
  90.5 42.9 %copy-start.1 = (f32[108,3]{1,0:T(8,128)S(1)}, f32[108,3]{1,0:T(8,128)}, u32[]{:S(2)}) copy-start(f32[108,3]{1,0:T(8,128)} %copy-done) | copy-start | bytes 3892
  111.8 8.4 %copy-start.38 = (f32[512]{0:T(512)}, f32[512]{0:T(512)S(1)}, u32[]{:S(2)}) copy-start(f32[512]{0:T(512)S(1)} %fusion.37) | copy-start | bytes 6148
  181.0 22.0 %copy-start.30 = (f32[8,512]{1,0:T(8,128)S(1)}, f32[8,512]{1,0:T(8,128)}, u32[]{:S(2)}) copy-start(f32[8,512]{1,0:T(8,128)} %pair.2) | copy-start | bytes 49156
  181.0 22.0 %copy-start.39 = (f32[512]{0:T(512)S(1)}, f32[512]{0:T(512)}, u32[]{:S(2)}) copy-start(f32[512]{0:T(512)} %copy-done.38) | copy-start | bytes 6148
  (8 other events, 11.6 us)

commit v3 on v2

--- a/solution.py
+++ b/solution.py
@@ -221,6 +221,16 @@
     return wide, jnp.where(reach, spread(gap * plain), 0.0)
 
 
+def move(values, onehot):
+    rows = values.shape[0]
+    first = values.astype(jnp.bfloat16).astype(jnp.float32)
+    rest = values - first
+    second = rest.astype(jnp.bfloat16).astype(jnp.float32)
+    stacked = jnp.concatenate([first, second, rest - second], axis=0).astype(jnp.bfloat16)
+    moved = jnp.dot(stacked, onehot.astype(jnp.bfloat16), preferred_element_type=jnp.float32)
+    return moved[0:rows] + (moved[rows : 2 * rows] + moved[2 * rows : 3 * rows])
+
+
 def sort_kernel(own_ref, chunk_ref, column_ref, row_ref, rank_ref):
     slots = own_ref.shape[-1]
     own = own_ref[...]
@@ -244,9 +254,7 @@
         part_column = jnp.floor(rank_column * (1.0 / size))
         part_row = jnp.floor(rank_row * (1.0 / size))
     place = jnp.where(rank_column.astype(jnp.int32) == second, 1.0, 0.0)
-    ordered = jnp.dot(
-        own, place, precision=lax.Precision.HIGHEST, preferred_element_type=jnp.float32
-    )
+    ordered = move(own, place)
     row_ref[...] = ordered
     column_ref[...] = ordered.T
     for k in range(slots // LANES):
@@ -254,8 +262,11 @@
     rank_ref[...] = rank_row.astype(jnp.int32)
 
 
-def born_kernel(near_ref, own_ref, list_ref, count_ref, offset_ref, out_ref):
+def born_kernel(
+    near_ref, own_ref, list_ref, count_ref, offset_ref, out_ref, row_ref, held_ref
+):
     slots = own_ref.shape[0]
+    held_ref[...] = jnp.zeros_like(held_ref)
 
     def block(index, carry):
         base = pl.multiple_of(index * ROWS, ROWS)
@@ -280,12 +291,15 @@
         )
         own_screen = own_ref[pl.ds(base, ROWS), 4:5]
         radius = own_ref[pl.ds(base, ROWS), 6:7]
-        out_ref[pl.ds(base, ROWS), :] = radius + (
-            jnp.sum(summed, axis=1, keepdims=True) - own_screen
-        )
+        found = radius + (jnp.sum(summed, axis=1, keepdims=True) - own_screen)
+        out_ref[pl.ds(base, ROWS), :] = found
+        held_ref[pl.ds(base, ROWS), 0:1] = found
         return carry
 
     lax.fori_loop(0, slots // ROWS, block, 0)
+    turned = held_ref[...].T
+    for piece in range(slots // LANES):
+        row_ref[piece] = turned[0:1, piece * LANES : (piece + 1) * LANES]
 
 
 def force_kernel(
@@ -337,9 +351,7 @@
     force = held_ref[...].T + scale * fit_ref[...]
     slot = lax.broadcasted_iota(jnp.int32, (slots, slots), 0)
     back = jnp.where(slot == rank_ref[...], 1.0, 0.0)
-    out_ref[...] = jnp.dot(
-        force, back, precision=lax.Precision.HIGHEST, preferred_element_type=jnp.float32
-    )
+    out_ref[...] = move(force, back)
 
 
 def halves(value):
@@ -481,25 +493,40 @@
         out_ref[axis : axis + 1, :] = mass * force[axis]
 
 
+def frame_kernel(dims, cube_ref, out_ref):
+    reaches = (REACH, PAD, PAD)
+
+    def span(side, axis):
+        length, reach = dims[axis], reaches[axis]
+        if side == 0:
+            return slice(length - reach, length), slice(0, reach)
+        if side == 1:
+            return slice(0, length), slice(reach, reach + length)
+        return slice(0, reach), slice(reach + length, length + 2 * reach)
+
+    for a in range(3):
+        from_x, to_x = span(a, 0)
+        for b in range(3):
+            from_y, to_y = span(b, 1)
+            out_ref[to_x, to_y, :] = jnp.concatenate(
+                [
+                    cube_ref[a * 9 + b * 3 + c, from_x, from_y, :][:, :, span(c, 2)[0]]
+                    for c in range(3)
+                ],
+                axis=2,
+            )
+
+
 def frame_map(bricks, dims):
-    reaches = (REACH, PAD, PAD)
-    cube = bricks.reshape((3, 3, 3) + dims)
-
-    def join(parts, axis):
-        length = dims[axis]
-        return jnp.concatenate(
-            [
-                lax.slice_in_dim(parts[0], length - reaches[axis], length, axis=axis),
-                parts[1],
-                lax.slice_in_dim(parts[2], 0, reaches[axis], axis=axis),
-            ],
-            axis=axis,
-        )
-
-    return join(
-        [join([join([cube[a, b, c] for c in range(3)], 2) for b in range(3)], 1) for a in range(3)],
-        0,
-    )
+    return pl.pallas_call(
+        functools.partial(frame_kernel, dims),
+        out_shape=jax.ShapeDtypeStruct(
+            (dims[0] + 2 * REACH, dims[1] + 2 * PAD, dims[2] + 2 * PAD), jnp.float32
+        ),
+        in_specs=[VMEM],
+        out_specs=VMEM,
+        name="frame",
+    )(bricks.reshape((27,) + dims))
 
 
 def active_lists(near, columns, offsets):
@@ -584,11 +611,15 @@
             (near,) = exchange([chunks], None, 1)
         near = near.reshape(27 * pieces, 8, LANES)
         lists, counts = active_lists(near, columns, offsets)
-        radius = pl.pallas_call(
+        radius, radius_rows = pl.pallas_call(
             born_kernel,
-            out_shape=jax.ShapeDtypeStruct((slots, 1), jnp.float32),
+            out_shape=[
+                jax.ShapeDtypeStruct((slots, 1), jnp.float32),
+                jax.ShapeDtypeStruct((pieces, 1, LANES), jnp.float32),
+            ],
             in_specs=[VMEM, VMEM, SMEM, SMEM, SMEM],
-            out_specs=VMEM,
+            out_specs=[VMEM, VMEM],
+            scratch_shapes=[pltpu.VMEM((slots, 8), jnp.float32)],
             name="born",
         )(near, columns, lists, counts, offsets)
         evolved, part = pl.pallas_call(
@@ -608,7 +639,7 @@
             name="evolve",
         )(near, exp_map, place)
         near_radius, halo, parts = exchange(
-            [radius.reshape(pieces, 1, LANES), evolved.reshape(-1, LANES)], part, 2
+            [radius_rows, evolved.reshape(-1, LANES)], part, 2
         )
         near_radius = near_radius.reshape(27 * pieces, 1, LANES)
         wide = frame_map(halo, dims)

time: 209 us -> 196 us (0.938)
  the two profiles are of different devices: /device:TPU:20 before, /device:TPU:9 now
where the time goes in v3:
time: 196 us; the launch traced here: 193 us
  Pallas kernels  144 us (73%)
  local copies, waits for them, and re-layouts  23.9 us (12%)
  other arithmetic  19.3 us (10%)
  between operations  5.39 us (3%)
    pallas_call x4, Pallas kernels, exchange(): pl.pallas_call(functools.partial(exchange_kernel, sizes, count, everyone)...  42.5 us
    pallas_call x2, Pallas kernels, on_device(): pl.pallas_call(functools.partial(force_kernel, scale), out_shape=jax.Shap...  36 us
    pallas_call x2, Pallas kernels, on_device(): pl.pallas_call(born_kernel, out_shape=[jax.ShapeDtypeStruct((slots, 1), j...  26.2 us
    pallas_call x2, Pallas kernels, on_device(): pl.pallas_call(functools.partial(evolved_kernel, dims, sizes), out_shape=...  18.4 us
    pallas_call x3, Pallas kernels, frame_map(): pl.pallas_call(functools.partial(frame_kernel, dims), out_shape=jax.Shape...  9.52 us
    reshape x3, local copies, waits for them, and re-layouts, frame_map(): bricks.reshape((27,) + dims)  9.46 us
    pallas_call x2, Pallas kernels, on_device(): pl.pallas_call(sort_kernel, out_shape=[jax.ShapeDtypeStruct((pieces, 8, L...  6.13 us
    pallas_call x2, Pallas kernels, on_device(): pl.pallas_call(functools.partial(fit_kernel, dims, sizes), out_shape=jax....  5.23 us

profile of v3, /device:TPU:9, one launch (start us, length us, event | category | flops | bytes accessed | tf_op | source)
XLA Modules:
  0.0 192.9 jit_solution(7805654464096845650)
XLA Ops:
  5.5 1.6 reshape.295.refs_1_
  7.2 3.1 %sort.2 = (f32[4,8,128]{2,1,0:T(8,128)}, f32[512,8]{1,0:T(8,128)}, f32[8,512]{1,0:T(8,128)}, s32[1,512]{1,0:T(1,128)}) custom-call(f32[8,512]{1,0:T(8,128)} %concatenate.19.own_ref), custom_call_target="tpu_custom_call" | custom-call | tf_op jit(solution)/shard_map/sort/pallas_call | solution.py:595
  11.5 1.1 select_reduce_fusion.5
  12.8 12.1 %exchange0.1 = (f32[27,4,8,128]{3,2,1,0:T(8,128)}, f32[27,32,128]{2,1,0:T(8,128)}) custom-call(f32[4,8,128]{2,1,0:T(8,128)} %get-tuple-element.27.refs_0_, f32[32,128]{1,0:T(8,128)} %reshape.295.refs_1_), custom_call_target="tpu_custom_call" | custom-call | tf_op jit(solution)/shard_map/exchange0/pallas_call | solution.py:180
  24.8 1.1 slice_compare_fusion.1
  26.0 1.5 select_reduce_fusion.9
  29.7 9.2 %evolve.2 = (f32[16,16,16]{2,1,0:T(8,128)}, f32[1,128]{1,0:T(1,128)}) custom-call(f32[108,8,128]{2,1,0:T(8,128)} %bitcast.64, f32[16,16,16]{2,1,0:T(8,128)} %map_ref.3, s32[1,3]{1,0:T(1,128)} %add_bitcast_fusion.place_ref), custom_call_target="tpu_custom_call" | custom-call | tf_op jit(solution)/shard_map/evolve/pallas_call | solution.py:625
  38.9 1.6 reshape.299.refs_1_
  40.5 13.1 %born.2 = (f32[512,1]{1,0:T(8,128)}, f32[4,1,128]{2,1,0:T(1,128)}) custom-call(f32[108,8,128]{2,1,0:T(8,128)} %bitcast.65, f32[512,8]{1,0:T(8,128)} %get-tuple-element.29.own_ref, s32[8,108]{1,0:T(8,128)} %select_reduce_fusion.1.list_ref, s32[1,8]{1,0:T(1,128)} %bitcast.76, f32[108,3]{1,0:T(8,128)} %copy-done.1), custom_call_target="tpu_custom_call" | custom-call | tf_op jit(solution)/shard_map/born/pallas_call | solution.py:614
  53.6 11.8 %exchange2.2 = (f32[27,4,1,128]{3,2,1,0:T(1,128)}, f32[27,32,128]{2,1,0:T(8,128)}, f32[32,1,128]{2,1,0:T(1,128)}) custom-call(f32[4,1,128]{2,1,0:T(1,128)} %get-tuple-element.30.refs_0_, f32[32,128]{1,0:T(8,128)} %reshape.299.refs_1_, f32[1,128]{1,0:T(1,128)} %get-tuple-element.32.refs_2_), custom_call_target="tpu_custom_call" | custom-call | tf_op jit(solution)/shard_map/exchange2/pallas_call | solution.py:180
  68.9 3.3 %reshape.302.cube_ref = f32[27,16,16,16]{3,2,1,0:T(8,128)} reshape(f32[27,32,128]{2,1,0:T(8,128)} %get-tuple-element.38) | data formatting | bytes 884736 | tf_op jit(solution)/shard_map/reshape | solution.py:529
  72.2 3.2 %frame.4 = f32[26,32,32]{2,1,0:T(8,128)} custom-call(f32[27,16,16,16]{3,2,1,0:T(8,128)} %reshape.302.cube_ref), custom_call_target="tpu_custom_call" | custom-call | tf_op jit(solution)/shard_map/frame/pallas_call | solution.py:521
  75.3 2.8 %reshape.301.cube_ref = f32[27,16,16,16]{3,2,1,0:T(8,128)} reshape(f32[27,32,128]{2,1,0:T(8,128)S(1)} %copy-done.4) | data formatting | bytes 884736 | tf_op jit(solution)/shard_map/reshape | solution.py:529
  78.2 3.2 %frame.3 = f32[26,32,32]{2,1,0:T(8,128)} custom-call(f32[27,16,16,16]{3,2,1,0:T(8,128)} %reshape.301.cube_ref), custom_call_target="tpu_custom_call" | custom-call | tf_op jit(solution)/shard_map/frame/pallas_call | solution.py:521
  81.4 1.1 divide_subtract_fusion.1
  83.5 2.6 %fit.2.fit_ref = f32[8,512]{1,0:T(8,128)} custom-call(f32[8,512]{1,0:T(8,128)} %get-tuple-element.35.own_ref, s32[1,3]{1,0:T(1,128)} %add_bitcast_fusion.place_ref, bf16[832,96]{1,0:T(8,128)(2,1)} %pad_maximum_fusion.sens_ref), custom_call_target="tpu_custom_call" | custom-call | tf_op jit(solution)/shard_map/fit/pallas_call | solution.py:655
  86.1 18.0 %pair.2 = f32[8,512]{1,0:T(8,128)} custom-call(f32[108,8,128]{2,1,0:T(8,128)} %bitcast.66, f32[108,1,128]{2,1,0:T(1,128)} %bitcast.74, f32[512,8]{1,0:T(8,128)} %get-tuple-element.29.own_ref, f32[512,1]{1,0:T(8,128)} %get-tuple-element.34.radius_ref, f32[8,512]{1,0:T(8,128)} %fit.2.fit_ref, s32[1,512]{1,0:T(1,128)} %get-tuple-element.39.rank_ref, ...), custom_call_target="tpu_custom_call" | custom-call | tf_op jit(solution)/shard_map/pair/pallas_call | solution.py:663
  105.4 3.1 %sort.3 = (f32[4,8,128]{2,1,0:T(8,128)}, f32[512,8]{1,0:T(8,128)}, f32[8,512]{1,0:T(8,128)}, s32[1,512]{1,0:T(1,128)}) custom-call(f32[8,512]{1,0:T(8,128)} %concatenate.21.own_ref), custom_call_target="tpu_custom_call" | custom-call | tf_op jit(solution)/shard_map/sort/pallas_call | solution.py:595
  108.5 1.1 slice.96
  109.7 1.1 select_reduce_fusion.3
  111.0 7.8 %exchange1.1 = f32[27,4,8,128]{3,2,1,0:T(8,128)} custom-call(f32[4,8,128]{2,1,0:T(8,128)} %get-tuple-element.40.refs_0_), custom_call_target="tpu_custom_call" | custom-call | tf_op jit(solution)/shard_map/exchange1/pallas_call | solution.py:180
  118.8 1.1 slice_compare_fusion
  120.0 1.5 select_reduce_fusion.7
  123.7 9.2 %evolve.3 = (f32[16,16,16]{2,1,0:T(8,128)}, f32[1,128]{1,0:T(1,128)}) custom-call(f32[108,8,128]{2,1,0:T(8,128)} %bitcast.59, f32[16,16,16]{2,1,0:T(8,128)} %map_ref.3, s32[1,3]{1,0:T(1,128)} %add_bitcast_fusion.place_ref), custom_call_target="tpu_custom_call" | custom-call | tf_op jit(solution)/shard_map/evolve/pallas_call | solution.py:625
  132.9 1.6 reshape.306.refs_1_
  134.5 13.1 %born.3 = (f32[512,1]{1,0:T(8,128)}, f32[4,1,128]{2,1,0:T(1,128)}) custom-call(f32[108,8,128]{2,1,0:T(8,128)} %bitcast.60, f32[512,8]{1,0:T(8,128)} %get-tuple-element.41.own_ref, s32[8,108]{1,0:T(8,128)} %select_reduce_fusion.list_ref, s32[1,8]{1,0:T(1,128)} %bitcast.78, f32[108,3]{1,0:T(8,128)} %copy-done.1), custom_call_target="tpu_custom_call" | custom-call | tf_op jit(solution)/shard_map/born/pallas_call | solution.py:614
  147.6 10.8 %exchange2.3 = (f32[27,4,1,128]{3,2,1,0:T(1,128)}, f32[27,32,128]{2,1,0:T(8,128)}, f32[32,1,128]{2,1,0:T(1,128)}) custom-call(f32[4,1,128]{2,1,0:T(1,128)} %get-tuple-element.42.refs_0_, f32[32,128]{1,0:T(8,128)} %reshape.306.refs_1_, f32[1,128]{1,0:T(1,128)} %get-tuple-element.44.refs_2_), custom_call_target="tpu_custom_call" | custom-call | tf_op jit(solution)/shard_map/exchange2/pallas_call | solution.py:180
  161.8 3.3 %reshape.308.cube_ref = f32[27,16,16,16]{3,2,1,0:T(8,128)} reshape(f32[27,32,128]{2,1,0:T(8,128)} %get-tuple-element.49) | data formatting | bytes 884736 | tf_op jit(solution)/shard_map/reshape | solution.py:529
  165.1 3.2 %frame.5 = f32[26,32,32]{2,1,0:T(8,128)} custom-call(f32[27,16,16,16]{3,2,1,0:T(8,128)} %reshape.308.cube_ref), custom_call_target="tpu_custom_call" | custom-call | tf_op jit(solution)/shard_map/frame/pallas_call | solution.py:521
  168.2 1.1 divide_subtract_fusion
  170.3 2.6 %fit.3.fit_ref = f32[8,512]{1,0:T(8,128)} custom-call(f32[8,512]{1,0:T(8,128)} %get-tuple-element.47.own_ref, s32[1,3]{1,0:T(1,128)} %add_bitcast_fusion.place_ref, bf16[832,96]{1,0:T(8,128)(2,1)} %pad_maximum_fusion.1.sens_ref), custom_call_target="tpu_custom_call" | custom-call | tf_op jit(solution)/shard_map/fit/pallas_call | solution.py:655
  172.9 18.0 %pair.3 = f32[8,512]{1,0:T(8,128)} custom-call(f32[108,8,128]{2,1,0:T(8,128)} %bitcast.61, f32[108,1,128]{2,1,0:T(1,128)} %bitcast.73, f32[512,8]{1,0:T(8,128)} %get-tuple-element.41.own_ref, f32[512,1]{1,0:T(8,128)} %get-tuple-element.46.radius_ref, f32[8,512]{1,0:T(8,128)} %fit.3.fit_ref, s32[1,512]{1,0:T(1,128)} %get-tuple-element.50.rank_ref, ...), custom_call_target="tpu_custom_call" | custom-call | tf_op jit(solution)/shard_map/pair/pallas_call | solution.py:663
  (69 shorter events, 18.7 us)
Async XLA Ops:
  7.2 33.3 %copy-start.1 = (f32[108,3]{1,0:T(8,128)}, f32[108,3]{1,0:T(8,128)S(1)}, u32[]{:S(2)}) copy-start(f32[108,3]{1,0:T(8,128)S(1)} %broadcast_multiply_fusion.offset_ref) | copy-start | bytes 3892
  68.8 6.5 %copy-start.4 = (f32[27,32,128]{2,1,0:T(8,128)S(1)}, f32[27,32,128]{2,1,0:T(8,128)}, u32[]{:S(2)}) copy-start(f32[27,32,128]{2,1,0:T(8,128)} %get-tuple-element.36) | copy-start | bytes 1327108
  75.3 6.0 %copy-start.3 = (f32[26,32,32]{2,1,0:T(8,128)S(1)}, f32[26,32,32]{2,1,0:T(8,128)}, u32[]{:S(2)}) copy-start(f32[26,32,32]{2,1,0:T(8,128)} %frame.4) | copy-start | bytes 319492
  78.2 25.9 %copy-start.6 = (f32[3,1,1,1,512]{4,3,2,1,0:T(1,128)S(1)}, f32[3,1,1,1,512]{4,3,2,1,0:T(1,128)}, u32[]{:S(2)}) copy-start(f32[3,1,1,1,512]{4,3,2,1,0:T(1,128)} %param.7) | copy-start | bytes 18436
  81.4 38.6 %copy-start.2 = (f32[108,3]{1,0:T(8,128)S(1)}, f32[108,3]{1,0:T(8,128)}, u32[]{:S(2)}) copy-start(f32[108,3]{1,0:T(8,128)} %copy-done.1) | copy-start | bytes 3892
  161.8 6.5 %copy-start = (f32[26,32,32]{2,1,0:T(8,128)S(1)}, f32[26,32,32]{2,1,0:T(8,128)}, u32[]{:S(2)}) copy-start(f32[26,32,32]{2,1,0:T(8,128)} %frame.3) | copy-start | bytes 319492
  165.1 25.9 %copy-start.5 = (f32[8,512]{1,0:T(8,128)S(1)}, f32[8,512]{1,0:T(8,128)}, u32[]{:S(2)}) copy-start(f32[8,512]{1,0:T(8,128)} %pair.2) | copy-start | bytes 49156

commit v4 on v3

--- a/solution.py
+++ b/solution.py
@@ -275,19 +275,27 @@
             for k in range(3)
         ]
 
+        many = count_ref[0, index]
+
         def visit(step, summed):
-            number = list_ref[index, step]
+            following = 2 * step + 1
+            more = following < many
+            number = jnp.where(more, list_ref[index, following], 13 * (slots // LANES))
+            summed = meet(list_ref[index, 2 * step], 1.0, summed)
+            return meet(number, jnp.where(more, 1.0, 0.0), summed)
+
+        def meet(number, factor, summed):
             squared = None
             for axis in range(3):
                 row = near_ref[number, axis : axis + 1, :] + offset_ref[number, axis]
                 gap = own[axis] - row
                 squared = gap * gap if squared is None else squared + gap * gap
             smooth = jnp.maximum(1.0 - squared * (1.0 / (CUTOFF * CUTOFF)), 0.0)
-            weight = near_ref[number, 4:5, :]
+            weight = near_ref[number, 4:5, :] * factor
             return summed + jnp.exp(squared * -0.125) * (smooth * smooth) * weight
 
         summed = lax.fori_loop(
-            0, count_ref[0, index], visit, jnp.zeros((ROWS, LANES), jnp.float32)
+            0, (many + 1) // 2, visit, jnp.zeros((ROWS, LANES), jnp.float32)
         )
         own_screen = own_ref[pl.ds(base, ROWS), 4:5]
         radius = own_ref[pl.ds(base, ROWS), 6:7]
@@ -318,8 +326,16 @@
         radius = jnp.broadcast_to(radius_ref[pl.ds(base, ROWS), :], (ROWS, LANES))
         inverse_radius = -0.25 / radius
 
+        many = count_ref[0, index]
+
         def visit(step, summed):
-            number = list_ref[index, step]
+            following = 2 * step + 1
+            more = following < many
+            number = jnp.where(more, list_ref[index, following], 13 * (slots // LANES))
+            summed = meet(list_ref[index, 2 * step], 1.0, summed)
+            return meet(number, jnp.where(more, 1.0, 0.0), summed)
+
+        def meet(number, factor, summed):
             squared = None
             gaps = []
             for axis in range(3):
@@ -329,7 +345,7 @@
                 squared = gap * gap if squared is None else squared + gap * gap
             smooth = jnp.maximum(1.0 - squared * (1.0 / (CUTOFF * CUTOFF)), 0.0)
             near_radius = radii_ref[number]
-            charge = near_ref[number, 3:4, :]
+            charge = near_ref[number, 3:4, :] * factor
             fading = jnp.exp(squared * (inverse_radius * (1.0 / near_radius)))
             inverse = lax.rsqrt(squared + (radius * near_radius) * fading)
             common = (charge * (smooth * inverse)) * (
@@ -339,7 +355,7 @@
             return tuple(total + common * gap for total, gap in zip(summed, gaps))
 
         zero = jnp.zeros((ROWS, LANES), jnp.float32)
-        summed = lax.fori_loop(0, count_ref[0, index], visit, (zero, zero, zero))
+        summed = lax.fori_loop(0, (many + 1) // 2, visit, (zero, zero, zero))
         charge = own_ref[pl.ds(base, ROWS), 3:4]
         for axis in range(3):
             held_ref[pl.ds(base, ROWS), axis : axis + 1] = -charge * jnp.sum(

time: 196 us -> 190 us (0.969)
  the two profiles are of different devices: /device:TPU:9 before, /device:TPU:20 now
where the time goes in v4:
time: 190 us; the launch traced here: 187 us
  Pallas kernels  138 us (73%)
  local copies, waits for them, and re-layouts  23.9 us (13%)
  other arithmetic  19.3 us (10%)
  between operations  5.39 us (3%)
    pallas_call x4, Pallas kernels, exchange(): pl.pallas_call(functools.partial(exchange_kernel, sizes, count, everyone)...  42.8 us
    pallas_call x2, Pallas kernels, on_device(): pl.pallas_call(functools.partial(force_kernel, scale), out_shape=jax.Shap...  33 us
    pallas_call x2, Pallas kernels, on_device(): pl.pallas_call(born_kernel, out_shape=[jax.ShapeDtypeStruct((slots, 1), j...  23.1 us
    pallas_call x2, Pallas kernels, on_device(): pl.pallas_call(functools.partial(evolved_kernel, dims, sizes), out_shape=...  18.4 us
    pallas_call x3, Pallas kernels, frame_map(): pl.pallas_call(functools.partial(frame_kernel, dims), out_shape=jax.Shape...  9.52 us
    reshape x3, local copies, waits for them, and re-layouts, frame_map(): bricks.reshape((27,) + dims)  9.46 us
    pallas_call x2, Pallas kernels, on_device(): pl.pallas_call(sort_kernel, out_shape=[jax.ShapeDtypeStruct((pieces, 8, L...  6.13 us
    pallas_call x2, Pallas kernels, on_device(): pl.pallas_call(functools.partial(fit_kernel, dims, sizes), out_shape=jax....  5.23 us

profile of v4, /device:TPU:20, one launch (start us, length us, event | category | flops | bytes accessed | tf_op | source)
XLA Modules:
  0.0 187.1 jit_solution(17903634590897425713)
XLA Ops:
  5.5 1.6 reshape.295.refs_1_
  7.2 3.1 %sort.2 = (f32[4,8,128]{2,1,0:T(8,128)}, f32[512,8]{1,0:T(8,128)}, f32[8,512]{1,0:T(8,128)}, s32[1,512]{1,0:T(1,128)}) custom-call(f32[8,512]{1,0:T(8,128)} %concatenate.19.own_ref), custom_call_target="tpu_custom_call" | custom-call | tf_op jit(solution)/shard_map/sort/pallas_call | solution.py:611
  10.3 1.1 slice.91
  11.5 1.1 select_reduce_fusion.5
  12.8 12.4 %exchange0.1 = (f32[27,4,8,128]{3,2,1,0:T(8,128)}, f32[27,32,128]{2,1,0:T(8,128)}) custom-call(f32[4,8,128]{2,1,0:T(8,128)} %get-tuple-element.27.refs_0_, f32[32,128]{1,0:T(8,128)} %reshape.295.refs_1_), custom_call_target="tpu_custom_call" | custom-call | tf_op jit(solution)/shard_map/exchange0/pallas_call | solution.py:180
  25.2 1.1 slice_compare_fusion.1
  26.3 1.5 select_reduce_fusion.9
  30.1 9.2 %evolve.2 = (f32[16,16,16]{2,1,0:T(8,128)}, f32[1,128]{1,0:T(1,128)}) custom-call(f32[108,8,128]{2,1,0:T(8,128)} %bitcast.64, f32[16,16,16]{2,1,0:T(8,128)} %map_ref.3, s32[1,3]{1,0:T(1,128)} %add_bitcast_fusion.place_ref), custom_call_target="tpu_custom_call" | custom-call | tf_op jit(solution)/shard_map/evolve/pallas_call | solution.py:641
  39.3 1.6 reshape.299.refs_1_
  40.9 11.5 %born.2 = (f32[512,1]{1,0:T(8,128)}, f32[4,1,128]{2,1,0:T(1,128)}) custom-call(f32[108,8,128]{2,1,0:T(8,128)} %bitcast.65, f32[512,8]{1,0:T(8,128)} %get-tuple-element.29.own_ref, s32[8,108]{1,0:T(8,128)} %select_reduce_fusion.1.list_ref, s32[1,8]{1,0:T(1,128)} %bitcast.76, f32[108,3]{1,0:T(8,128)} %copy-done.1), custom_call_target="tpu_custom_call" | custom-call | tf_op jit(solution)/shard_map/born/pallas_call | solution.py:630
  52.4 11.2 %exchange2.2 = (f32[27,4,1,128]{3,2,1,0:T(1,128)}, f32[27,32,128]{2,1,0:T(8,128)}, f32[32,1,128]{2,1,0:T(1,128)}) custom-call(f32[4,1,128]{2,1,0:T(1,128)} %get-tuple-element.30.refs_0_, f32[32,128]{1,0:T(8,128)} %reshape.299.refs_1_, f32[1,128]{1,0:T(1,128)} %get-tuple-element.32.refs_2_), custom_call_target="tpu_custom_call" | custom-call | tf_op jit(solution)/shard_map/exchange2/pallas_call | solution.py:180
  67.0 3.3 %reshape.302.cube_ref = f32[27,16,16,16]{3,2,1,0:T(8,128)} reshape(f32[27,32,128]{2,1,0:T(8,128)} %get-tuple-element.38) | data formatting | bytes 884736 | tf_op jit(solution)/shard_map/reshape | solution.py:545
  70.3 3.2 %frame.4 = f32[26,32,32]{2,1,0:T(8,128)} custom-call(f32[27,16,16,16]{3,2,1,0:T(8,128)} %reshape.302.cube_ref), custom_call_target="tpu_custom_call" | custom-call | tf_op jit(solution)/shard_map/frame/pallas_call | solution.py:537
  73.5 2.8 %reshape.301.cube_ref = f32[27,16,16,16]{3,2,1,0:T(8,128)} reshape(f32[27,32,128]{2,1,0:T(8,128)S(1)} %copy-done.4) | data formatting | bytes 884736 | tf_op jit(solution)/shard_map/reshape | solution.py:545
  76.3 3.2 %frame.3 = f32[26,32,32]{2,1,0:T(8,128)} custom-call(f32[27,16,16,16]{3,2,1,0:T(8,128)} %reshape.301.cube_ref), custom_call_target="tpu_custom_call" | custom-call | tf_op jit(solution)/shard_map/frame/pallas_call | solution.py:537
  79.5 1.1 divide_subtract_fusion.1
  81.6 2.6 %fit.2.fit_ref = f32[8,512]{1,0:T(8,128)} custom-call(f32[8,512]{1,0:T(8,128)} %get-tuple-element.35.own_ref, s32[1,3]{1,0:T(1,128)} %add_bitcast_fusion.place_ref, bf16[832,96]{1,0:T(8,128)(2,1)} %pad_maximum_fusion.sens_ref), custom_call_target="tpu_custom_call" | custom-call | tf_op jit(solution)/shard_map/fit/pallas_call | solution.py:671
  84.2 16.4 %pair.2 = f32[8,512]{1,0:T(8,128)} custom-call(f32[108,8,128]{2,1,0:T(8,128)} %bitcast.66, f32[108,1,128]{2,1,0:T(1,128)} %bitcast.74, f32[512,8]{1,0:T(8,128)} %get-tuple-element.29.own_ref, f32[512,1]{1,0:T(8,128)} %get-tuple-element.34.radius_ref, f32[8,512]{1,0:T(8,128)} %fit.2.fit_ref, s32[1,512]{1,0:T(1,128)} %get-tuple-element.39.rank_ref, ...), custom_call_target="tpu_custom_call" | custom-call | tf_op jit(solution)/shard_map/pair/pallas_call | solution.py:679
  101.9 3.1 %sort.3 = (f32[4,8,128]{2,1,0:T(8,128)}, f32[512,8]{1,0:T(8,128)}, f32[8,512]{1,0:T(8,128)}, s32[1,512]{1,0:T(1,128)}) custom-call(f32[8,512]{1,0:T(8,128)} %concatenate.21.own_ref), custom_call_target="tpu_custom_call" | custom-call | tf_op jit(solution)/shard_map/sort/pallas_call | solution.py:611
  106.2 1.1 select_reduce_fusion.3
  107.5 8.1 %exchange1.1 = f32[27,4,8,128]{3,2,1,0:T(8,128)} custom-call(f32[4,8,128]{2,1,0:T(8,128)} %get-tuple-element.40.refs_0_), custom_call_target="tpu_custom_call" | custom-call | tf_op jit(solution)/shard_map/exchange1/pallas_call | solution.py:180
  115.6 1.1 slice_compare_fusion
  116.8 1.5 select_reduce_fusion.7
  120.5 9.2 %evolve.3 = (f32[16,16,16]{2,1,0:T(8,128)}, f32[1,128]{1,0:T(1,128)}) custom-call(f32[108,8,128]{2,1,0:T(8,128)} %bitcast.59, f32[16,16,16]{2,1,0:T(8,128)} %map_ref.3, s32[1,3]{1,0:T(1,128)} %add_bitcast_fusion.place_ref), custom_call_target="tpu_custom_call" | custom-call | tf_op jit(solution)/shard_map/evolve/pallas_call | solution.py:641
  129.7 1.6 reshape.306.refs_1_
  131.3 11.6 %born.3 = (f32[512,1]{1,0:T(8,128)}, f32[4,1,128]{2,1,0:T(1,128)}) custom-call(f32[108,8,128]{2,1,0:T(8,128)} %bitcast.60, f32[512,8]{1,0:T(8,128)} %get-tuple-element.41.own_ref, s32[8,108]{1,0:T(8,128)} %select_reduce_fusion.list_ref, s32[1,8]{1,0:T(1,128)} %bitcast.78, f32[108,3]{1,0:T(8,128)} %copy-done.1), custom_call_target="tpu_custom_call" | custom-call | tf_op jit(solution)/shard_map/born/pallas_call | solution.py:630
  142.9 11.1 %exchange2.3 = (f32[27,4,1,128]{3,2,1,0:T(1,128)}, f32[27,32,128]{2,1,0:T(8,128)}, f32[32,1,128]{2,1,0:T(1,128)}) custom-call(f32[4,1,128]{2,1,0:T(1,128)} %get-tuple-element.42.refs_0_, f32[32,128]{1,0:T(8,128)} %reshape.306.refs_1_, f32[1,128]{1,0:T(1,128)} %get-tuple-element.44.refs_2_), custom_call_target="tpu_custom_call" | custom-call | tf_op jit(solution)/shard_map/exchange2/pallas_call | solution.py:180
  157.4 3.3 %reshape.308.cube_ref = f32[27,16,16,16]{3,2,1,0:T(8,128)} reshape(f32[27,32,128]{2,1,0:T(8,128)} %get-tuple-element.49) | data formatting | bytes 884736 | tf_op jit(solution)/shard_map/reshape | solution.py:545
  160.8 3.2 %frame.5 = f32[26,32,32]{2,1,0:T(8,128)} custom-call(f32[27,16,16,16]{3,2,1,0:T(8,128)} %reshape.308.cube_ref), custom_call_target="tpu_custom_call" | custom-call | tf_op jit(solution)/shard_map/frame/pallas_call | solution.py:537
  163.9 1.1 divide_subtract_fusion
  166.0 2.6 %fit.3.fit_ref = f32[8,512]{1,0:T(8,128)} custom-call(f32[8,512]{1,0:T(8,128)} %get-tuple-element.47.own_ref, s32[1,3]{1,0:T(1,128)} %add_bitcast_fusion.place_ref, bf16[832,96]{1,0:T(8,128)(2,1)} %pad_maximum_fusion.1.sens_ref), custom_call_target="tpu_custom_call" | custom-call | tf_op jit(solution)/shard_map/fit/pallas_call | solution.py:671
  168.6 16.6 %pair.3 = f32[8,512]{1,0:T(8,128)} custom-call(f32[108,8,128]{2,1,0:T(8,128)} %bitcast.61, f32[108,1,128]{2,1,0:T(1,128)} %bitcast.73, f32[512,8]{1,0:T(8,128)} %get-tuple-element.41.own_ref, f32[512,1]{1,0:T(8,128)} %get-tuple-element.46.radius_ref, f32[8,512]{1,0:T(8,128)} %fit.3.fit_ref, s32[1,512]{1,0:T(1,128)} %get-tuple-element.50.rank_ref, ...), custom_call_target="tpu_custom_call" | custom-call | tf_op jit(solution)/shard_map/pair/pallas_call | solution.py:679
  (69 shorter events, 18.7 us)
Async XLA Ops:
  7.2 33.7 %copy-start.1 = (f32[108,3]{1,0:T(8,128)}, f32[108,3]{1,0:T(8,128)S(1)}, u32[]{:S(2)}) copy-start(f32[108,3]{1,0:T(8,128)S(1)} %broadcast_multiply_fusion.offset_ref) | copy-start | bytes 3892
  67.0 6.5 %copy-start.4 = (f32[27,32,128]{2,1,0:T(8,128)S(1)}, f32[27,32,128]{2,1,0:T(8,128)}, u32[]{:S(2)}) copy-start(f32[27,32,128]{2,1,0:T(8,128)} %get-tuple-element.36) | copy-start | bytes 1327108
  73.5 6.0 %copy-start.3 = (f32[26,32,32]{2,1,0:T(8,128)S(1)}, f32[26,32,32]{2,1,0:T(8,128)}, u32[]{:S(2)}) copy-start(f32[26,32,32]{2,1,0:T(8,128)} %frame.4) | copy-start | bytes 319492
  76.3 24.3 %copy-start.6 = (f32[3,1,1,1,512]{4,3,2,1,0:T(1,128)S(1)}, f32[3,1,1,1,512]{4,3,2,1,0:T(1,128)}, u32[]{:S(2)}) copy-start(f32[3,1,1,1,512]{4,3,2,1,0:T(1,128)} %param.7) | copy-start | bytes 18436
  79.5 37.3 %copy-start.2 = (f32[108,3]{1,0:T(8,128)S(1)}, f32[108,3]{1,0:T(8,128)}, u32[]{:S(2)}) copy-start(f32[108,3]{1,0:T(8,128)} %copy-done.1) | copy-start | bytes 3892
  157.4 6.5 %copy-start = (f32[26,32,32]{2,1,0:T(8,128)S(1)}, f32[26,32,32]{2,1,0:T(8,128)}, u32[]{:S(2)}) copy-start(f32[26,32,32]{2,1,0:T(8,128)} %frame.3) | copy-start | bytes 319492
  160.8 24.4 %copy-start.5 = (f32[8,512]{1,0:T(8,128)S(1)}, f32[8,512]{1,0:T(8,128)}, u32[]{:S(2)}) copy-start(f32[8,512]{1,0:T(8,128)} %pair.2) | copy-start | bytes 49156
